TPU v7x, 256 devices: a whole 4x4x8 slice. The times are simulated.
256 devices in a mesh: row: 32 (over z, x), col: 8 (over y, core).
Axes of the slice: x: 4, y: 4, z: 8, core: 2. Of those that a mesh axis runs over, the one named last changes fastest.
Arguments:
- trail_grad: bfloat16 [16384, 16384], P('row', 'col'), may hold values from -6 to 6
- panel_factor: bfloat16 [16384, 1024], P('col'), may hold values from -0.046875 to 0.046875
- cross_factor: bfloat16 [512, 512], replicated, may hold values from -0.25 to 0.25
- diag_factor: bfloat16 [2, 512, 512], replicated, may hold values from -1 to 3, as said below
- diag_inverse: float32 [2, 512, 512], replicated, may hold values from -2 to 2, as said below
- panel_grad: bfloat16 [16384, 1024], P('row'), may hold values from -6 to 6
- cross_grad: bfloat16 [512, 512], replicated, may hold values from -6 to 6
- diag_grad: bfloat16 [2, 512, 512], replicated, may hold values from -6 to 6
Outputs:
- panel_adj: float32 [16384, 1024], P('row', 'col')
- cross_adj: float32 [512, 512], P('col')
- diag_adj: float32 [2, 512, 512], P(None, 'col')
Inputs may be any that keep to these rules, and one draw needn't show every extreme that they name: Each diag_factor[p] is lower triangular with a positive diagonal. diag_inverse[p] is the float32 inverse of diag_factor[p], lower triangular.
All inputs are finite; a program needn't handle non-finite values.
Results may differ from a plain program's by a relative error of at most 0.0003.
Values may be sent and summed in bfloat16 or wider, within the bound.
A program may use at most 128 MiB of HBM per device.

v0:
```python
import jax
import jax.numpy as jnp
from jax import lax
from jax.sharding import Mesh
from jax.sharding import PartitionSpec as P

ROW = ("row_0", "row_1")


def broadcast(x, axis, root):
    return lax.dynamic_index_in_dim(lax.all_gather(x, axis), root, 0, keepdims=False)


def whole_of(x, axes, dim):
    for axis in reversed(axes):
        x = lax.all_gather(x, axis, axis=dim, tiled=True)
    return x


def gathered_total(x, axis):
    blocks = lax.all_gather(x, axis)
    return blocks.sum(axis=0)


def cut_along(x, dim, devices):
    before, after = (x.shape[:dim], x.shape[dim + 1 :])
    return jnp.moveaxis(x.reshape(*before, devices, -1, *after), dim, 0)


def summed_on_arrival(x, axis, dim):
    devices = lax.axis_size(axis)
    blocks = lax.all_to_all(cut_along(x, dim, devices), axis, 0, 0, tiled=True)
    return jnp.sum(blocks, axis=0)


def padded_to(lines, devices):
    spare = -len(lines) % devices
    return jnp.pad(lines, [(0, spare)] + [(0, 0)] * (lines.ndim - 1))


def laid_out(blocks, dim):
    blocks = jnp.moveaxis(blocks, 0, dim)
    lengths = blocks.shape
    return blocks.reshape(*lengths[:dim], lengths[dim] * lengths[dim + 1], *lengths[dim + 2 :])


def copy_for_each(x, axis):
    devices = lax.axis_size(axis)
    return lax.all_to_all(jnp.broadcast_to(x[None], (devices, *x.shape)), axis, 0, 0, tiled=True)


def gather_directly(x, axis, dim):
    return laid_out(copy_for_each(x, axis), dim)


def sum_by_parts(x, axes):
    own = summed_on_arrival(padded_to(x, lax.axis_size(axes)), axes, 0)
    whole = gather_directly(own, axes, 0)
    return whole[: len(x)].reshape(x.shape)


def packed_total(arrays, axis):
    vector, at, finished = (jnp.concatenate([a.reshape(-1) for a in arrays]), 0, [])
    subtotal = sum_by_parts(vector, axis)
    for a in arrays:
        finished.append(subtotal[at : at + a.size].reshape(a.shape))
        at += a.size
    return tuple(finished)


def total_of(x, axes):
    lines = x.reshape(-1, x.shape[-1])
    padded = padded_to(lines, lax.axis_size(axes))
    whole = gather_directly(summed_on_arrival(padded, axes, 0), axes, 0)
    return lax.slice_in_dim(whole, 0, len(lines)).reshape(x.shape)


def halve_lower(matrix):
    size = matrix.shape[0]
    row_ids = lax.broadcasted_iota(jnp.int32, (size, size), 0)
    col_ids = lax.broadcasted_iota(jnp.int32, (size, size), 1)
    return jnp.where(
        col_ids < row_ids,
        matrix,
        jnp.where(col_ids == row_ids, matrix * 0.5, jnp.zeros_like(matrix)),
    )


def inner_rows(left_mat, right_mat):
    return lax.dot_general(
        left_mat, right_mat, (((0,), (0,)), ((), ())), precision=lax.Precision.HIGHEST
    )


def block_adjoint(factor_block, inverse_block, gradient):
    product = inner_rows(factor_block.astype(jnp.float32), gradient)
    halved = halve_lower(product)
    symmetric = halved + halved.T
    inner = inner_rows(inverse_block, symmetric)
    return jnp.dot(inner, inverse_block, precision=lax.Precision.HIGHEST)


def shards(
    trail_grad,
    panel_factor,
    cross_factor,
    diag_factor,
    diag_inverse,
    panel_grad,
    cross_grad,
    diag_grad,
):
    highest = lax.Precision.HIGHEST
    panel_width = cross_factor.shape[0]
    rows_here, cols_here = trail_grad.shape
    stride = lax.axis_size(ROW) // lax.axis_size("col")
    row_id = lax.axis_index(ROW)
    col_id = lax.axis_index("col")
    row_glob = row_id * rows_here + lax.broadcasted_iota(jnp.int32, (rows_here, cols_here), 0)
    col_glob = col_id * cols_here + lax.broadcasted_iota(jnp.int32, (rows_here, cols_here), 1)
    filler = jnp.zeros_like(trail_grad)
    lower_half = jnp.where(
        col_glob < row_glob,
        trail_grad,
        jnp.where(col_glob == row_glob, trail_grad * jnp.bfloat16(0.5), filler),
    )
    own_offset = row_id % stride * rows_here
    own_piece = lax.dynamic_slice_in_dim(panel_factor, own_offset, rows_here, 0)
    factor_rows = broadcast(own_piece, "col", row_id // stride)
    strips = lax.all_to_all(lower_half, "col", split_axis=0, concat_axis=1, tiled=True)
    mirror_block = lax.all_to_all(strips, ROW, split_axis=1, concat_axis=0, tiled=True)
    piece_rows = rows_here // lax.axis_size("col")
    strip_factor = lax.dynamic_slice_in_dim(factor_rows, col_id * piece_rows, piece_rows, 0)
    strip_factor = whole_of(strip_factor, ROW, 0)

    def trailing(first_col, col_count):
        local_cols = panel_factor[:, first_col : first_col + col_count]
        direct_term = jnp.dot(lower_half, local_cols, preferred_element_type=jnp.float32)
        strip_cols = strip_factor[:, first_col : first_col + col_count]
        direct_term = direct_term + lax.dot_general(
            mirror_block, strip_cols, (((0,), (0,)), ((), ())), preferred_element_type=jnp.float32
        )
        direct_term = gathered_total(direct_term, "col")
        return direct_term

    factor_float = factor_rows.astype(jnp.float32)
    factor_zero = factor_float[:, :panel_width]
    factor_one = factor_float[:, panel_width:]
    grads = panel_grad.astype(jnp.float32)
    trail_one = trailing(panel_width, panel_width)
    adj_one = jnp.dot(grads[:, panel_width:] - trail_one, diag_inverse[1], precision=highest)
    row_sums = packed_total(
        (inner_rows(adj_one, factor_one), inner_rows(adj_one, factor_zero)), ROW
    )
    grad_one = diag_grad[1].astype(jnp.float32) - row_sums[0]
    block_one = block_adjoint(diag_factor[1], diag_inverse[1], grad_one)
    trail_zero = trailing(0, panel_width)
    cross_f = cross_factor.astype(jnp.float32)
    rest = grads[:, :panel_width] - trail_zero - jnp.dot(adj_one, cross_f, precision=highest)
    cross_rest = (
        cross_grad.astype(jnp.float32)
        - row_sums[1]
        - jnp.dot(block_one, cross_f, precision=highest)
    )
    adj_zero = jnp.dot(rest, diag_inverse[0], precision=highest)
    cross_adj = jnp.dot(cross_rest, diag_inverse[0], precision=highest)
    zero_sum = total_of(inner_rows(adj_zero, factor_zero), ROW)
    grad_zero = diag_grad[0].astype(jnp.float32) - zero_sum - inner_rows(cross_adj, cross_f)
    block_zero = block_adjoint(diag_factor[0], diag_inverse[0], grad_zero)
    full_panels = jnp.concatenate([adj_zero, adj_one], axis=1)
    out_cols = 2 * panel_width // lax.axis_size("col")
    out_rows = panel_width // lax.axis_size("col")
    panel_part = lax.dynamic_slice_in_dim(full_panels, col_id * out_cols, out_cols, 1)
    cross_part = lax.dynamic_slice_in_dim(cross_adj, col_id * out_rows, out_rows, 0)
    blocks = jnp.stack([block_zero, block_one])
    block_part = lax.dynamic_slice_in_dim(blocks, col_id * out_rows, out_rows, 1)
    return (panel_part, cross_part, block_part)


def solution(mesh):
    split = Mesh(mesh.devices.reshape(8, 4, mesh.shape["col"]), ("row_0", "row_1", "col"))
    return jax.shard_map(
        shards,
        mesh=split,
        in_specs=(P(ROW, "col"), P("col", None), P(), P(), P(), P(ROW, None), P(), P()),
        out_specs=(P(ROW, "col"), P("col", None), P(None, "col", None)),
        check_vma=False,
    )
```

profile of v0, /device:TPU:2, one launch (start us, length us, event | category | flops | bytes accessed | tf_op | source)
XLA Modules:
  0.0 469.4 jit_solution(4517538400826152772)
XLA Ops:
  7.3 2.4 constant_dynamic-slice_fusion.2
  9.7 0.0 all-gather.12.cloned.1.call-start
  9.8 55.4 %all-gather.10.cloned.1.call-done = bf16[4096,1024]{1,0:T(8,128)(2,1)} async-done(((bf16[512,1024]{1,0:T(8,128)(2,1)}), bf16[4096,1024]{1,0:T(8,128)(2,1)}) %all-gather.10.cloned.1.call-update) | async-done | bytes 8388624 | tf_op jit(solution)/shard_map/all_gather | solution.py:11
  65.2 0.9 constant_dynamic-slice_fusion.1
  66.1 13.8 %all-gather.1 = bf16[1,256,1024]{2,1,0:T(8,128)(2,1)} all-gather(bf16[1,64,1024]{2,1,0:T(8,128)(2,1)S(1)} %constant_dynamic-slice_fusion.1), channel_id=3, replica_groups=mesh['row_0'=8,'row_1'=4,'col'=8] {'row_1'}, dimensions={1}, use_global_device_ids=true | all-gather | bytes 655360 | tf_op jit(solution)/shard_map/all_gather | solution.py:16
  80.0 1.1 compare_select_fusion.1
  81.1 30.5 %all_to_all.60 = bf16[8,64,2048]{2,1,0:T(8,128)(2,1)S(1)} all-to-all(bf16[8,64,2048]{2,1,0:T(8,128)(2,1)S(1)} %bitcast.85), channel_id=1, replica_groups=mesh['row_0'=8,'row_1'=4,'col'=8] {'col'}, dimensions={0} | all-to-all | bytes 4194304 | tf_op jit(solution)/shard_map/all_to_all | solution.py:130
  111.6 1.2 copy.19
  112.8 2.6 all_to_all.45
  115.4 2.8 copy.20
  118.2 63.3 %all_to_all.61 = bf16[64,32,512]{2,0,1:T(8,128)(2,1)S(1)} all-to-all(bf16[64,32,512]{2,0,1:T(8,128)(2,1)S(1)} %copy.20), channel_id=1, replica_groups=mesh['row_0'=8,'row_1'=4,'col'=8] {'row_0','row_1'}, dimensions={1} | all-to-all | bytes 4194304 | tf_op jit(solution)/shard_map/all_to_all | solution.py:131
  181.5 3.0 fusion
  184.6 3.9 fusion.11
  188.4 0.2 all-gather.14.cloned.1.call-start
  188.7 3.0 fusion.2
  191.7 3.9 fusion.8
  195.7 1.6 convert_element_type.29
  197.3 1.4 dynamic-slice_bitcast_fusion
  198.7 38.8 %all-gather.16.cloned.1.call-done = f32[4096,512]{1,0:T(8,128)} async-done(((f32[512,512]{1,0:T(8,128)}), f32[4096,512]{1,0:T(8,128)}) %all-gather.16.cloned.1.call-update) | async-done | bytes 8388624 | tf_op jit(solution)/shard_map/all_gather | solution.py:21
  237.5 5.5 %reduce_sum.37 = f32[512,512]{1,0:T(8,128)} reduce(f32[8,512,512]{2,1,0:T(8,128)} %bitcast.84, f32[]{:T(128)} %constant.77.clone.1), dimensions={0}, to_apply=%region_1.2 | reduce | flops 1835008 | bytes 9437188 | tf_op jit(solution)/shard_map/reduce_sum | solution.py:22
  243.0 3.7 fusion.15
  246.7 2.0 fusion.47
  248.7 2.5 concatenate.12
  251.2 2.0 fusion.61
  253.2 2.8 concatenate.13
  256.0 1.4 pad_maximum_fusion
  257.4 3.6 all_to_all.49
  261.0 10.6 %all-to-all-start.2 = ((f32[32,1,16384]{2,1,0:T(1,128)}), f32[32,1,16384]{2,1,0:T(1,128)}, u32[]{:S(2)}, u32[]{:S(2)}) async-start(f32[32,1,16384]{2,1,0:T(1,128)} %all_to_all.49), calls=%async_computation.2 | async-start | bytes 4194304 | tf_op jit(solution)/shard_map/all_to_all | solution.py:32
  271.6 20.2 %all-gather.14.cloned.1.call-done = f32[4096,512]{1,0:T(8,128)} async-done(((f32[512,512]{1,0:T(8,128)}), f32[4096,512]{1,0:T(8,128)}) %all-gather.14.cloned.1.call-update) | async-done | bytes 8388624 | tf_op jit(solution)/shard_map/all_gather | solution.py:21
  291.8 4.5 reduce_sum.36
  296.3 2.4 convolution_subtract_fusion.2
  298.7 1.9 fusion.28
  300.6 2.0 fusion.59
  302.6 18.5 %all-to-all-done.2 = f32[32,1,16384]{2,1,0:T(1,128)} async-done(((f32[32,1,16384]{2,1,0:T(1,128)}), f32[32,1,16384]{2,1,0:T(1,128)}, u32[]{:S(2)}, u32[]{:S(2)}) %all-to-all-start.2) | async-done | bytes 2097184 | tf_op jit(solution)/shard_map/all_to_all | solution.py:32
  321.1 6.3 %all-to-all-start.4 = ((f32[32,16,512]{2,1,0:T(8,128)}), f32[32,16,512]{2,1,0:T(8,128)}, u32[]{:S(2)}, u32[]{:S(2)}) async-start(f32[32,16,512]{2,1,0:T(8,128)} %bitcast.89), calls=%async_computation.4 | async-start | bytes 2097152 | tf_op jit(solution)/shard_map/all_to_all | solution.py:32
  327.4 3.0 reduce_sum.38
  330.4 25.2 %all-to-all-done.4 = f32[32,16,512]{2,1,0:T(8,128)} async-done(((f32[32,16,512]{2,1,0:T(8,128)}), f32[32,16,512]{2,1,0:T(8,128)}, u32[]{:S(2)}, u32[]{:S(2)}) %all-to-all-start.4) | async-done | bytes 1048608 | tf_op jit(solution)/shard_map/all_to_all | solution.py:32
  355.6 3.2 broadcast_in_dim.7
  358.8 5.6 %all-to-all-start.3 = ((f32[32,1,16384]{2,1,0:T(1,128)}), f32[32,1,16384]{2,1,0:T(1,128)}, u32[]{:S(2)}, u32[]{:S(2)}) async-start(f32[32,1,16384]{2,1,0:T(1,128)} %broadcast_in_dim.7), calls=%async_computation.3 | async-start | bytes 4194304 | tf_op jit(solution)/shard_map/all_to_all | solution.py:49
  364.4 2.2 slice_convert_fusion
  366.5 3.5 reshape.67
  370.0 0.1 fusion.64
  370.1 0.8 copy.23
  370.9 1.4 reduce_sum.39
  372.3 40.9 %all-to-all-done.3 = f32[32,1,16384]{2,1,0:T(1,128)} async-done(((f32[32,1,16384]{2,1,0:T(1,128)}), f32[32,1,16384]{2,1,0:T(1,128)}, u32[]{:S(2)}, u32[]{:S(2)}) %all-to-all-start.3) | async-done | bytes 2097184 | tf_op jit(solution)/shard_map/all_to_all | solution.py:49
  413.2 1.1 broadcast_in_dim.8
  414.3 6.7 %all-to-all-start.5 = ((f32[32,16,512]{2,1,0:T(8,128)}), f32[32,16,512]{2,1,0:T(8,128)}, u32[]{:S(2)}, u32[]{:S(2)}) async-start(f32[32,16,512]{2,1,0:T(8,128)} %broadcast_in_dim.8), calls=%async_computation.5 | async-start | bytes 2097152 | tf_op jit(solution)/shard_map/all_to_all | solution.py:49
  421.0 8.5 %slice_reduce_fusion = (f32[16,16384]{1,0:T(8,128)}, f32[16,16384]{1,0:T(8,128)S(1)}) fusion(f32[32,1,16384]{2,1,0:T(1,128)} %all-to-all-done.3, f32[16,1,16384]{2,1,0:T(1,128)S(1)} %copy-done.11), kind=kLoop, calls=%fused_computation.23 | loop fusion | flops 262144 | bytes 5242880 | tf_op jit(solution)/shard_map/slice | solution.py:66
  429.5 2.4 reshape.64
  431.9 1.2 sub.39
  433.1 3.5 fusion.51
  436.6 2.5 copy.21
  439.1 3.5 fusion.22
  442.7 1.9 fusion.30
  444.6 1.0 convolution_subtract_fusion.1
  445.6 1.8 fusion.26
  447.4 1.0 copy-done.10
  448.4 0.7 constant_dynamic-slice_fusion
  449.1 2.8 convolution_subtract_fusion
  451.9 2.0 fusion.49
  453.9 2.5 copy.22
  456.4 3.7 fusion.18
  460.1 1.9 convolution_bitcast_fusion
  462.0 0.7 fusion.63
  (45 shorter events, 0.2 us)
Async XLA Ops:
  7.2 289.1 %copy-start = (bf16[512,512]{1,0:T(8,128)(2,1)S(1)}, bf16[512,512]{1,0:T(8,128)(2,1)}, u32[]{:S(2)}) copy-start(bf16[512,512]{1,0:T(8,128)(2,1)} %param.10) | copy-start | bytes 1572868
  7.2 58.0 %all-gather.10.cloned.1.call-start = ((), (), s32[]{:S(2)}) async-start(), calls=%async_computation.6 | async-start | bytes 9437184 | tf_op jit(solution)/shard_map/all_gather | solution.py:11
  7.2 72.8 %copy-start.14 = (bf16[512,2048]{1,0:T(8,128)(2,1)S(1)}, bf16[512,2048]{1,0:T(8,128)(2,1)}, u32[]{:S(2)}) copy-start(bf16[512,2048]{1,0:T(8,128)(2,1)} %param.8) | copy-start | bytes 6291460
  9.7 171.8 %all-gather.12.cloned.1.call-start = ((), (), s32[]{:S(2)}) async-start(), calls=%async_computation.7 | async-start | bytes 4718592 | tf_op jit(solution)/shard_map/all_gather | solution.py:16
  79.9 157.6 %all-gather.16.cloned.1.call-start = ((), (), s32[]{:S(2)}) async-start(), calls=%async_computation.9 | async-start | bytes 9437184 | tf_op jit(solution)/shard_map/all_gather | solution.py:21
  81.1 30.5 %copy-start.5 = (bf16[512,2048]{1,0:T(8,128)(2,1)}, bf16[512,2048]{1,0:T(8,128)(2,1)S(1)}, u32[]{:S(2)}) copy-start(bf16[512,2048]{1,0:T(8,128)(2,1)S(1)} %compare_select_fusion.1) | copy-start | bytes 6291460
  181.5 3.0 copy-start.6
  188.4 103.3 %all-gather.14.cloned.1.call-start = ((), (), s32[]{:S(2)}) async-start(), calls=%async_computation.8 | async-start | bytes 9437184 | tf_op jit(solution)/shard_map/all_gather | solution.py:21
  188.7 3.0 copy-start.7
  191.7 4.0 copy-start.15
  198.7 52.5 %copy-start.8 = (bf16[512,1024]{1,0:T(8,128)(2,1)}, bf16[512,1024]{1,0:T(8,128)(2,1)S(1)}, u32[]{:S(2)}) copy-start(bf16[512,1024]{1,0:T(8,128)(2,1)S(1)} %dynamic-slice_bitcast_fusion) | copy-start | bytes 3145732
  253.2 2.8 copy-start.13
  261.0 60.1 %all-to-all-start.2 = ((f32[32,1,16384]{2,1,0:T(1,128)}), f32[32,1,16384]{2,1,0:T(1,128)}, u32[]{:S(2)}, u32[]{:S(2)}) async-start(f32[32,1,16384]{2,1,0:T(1,128)} %all_to_all.49), calls=%async_computation.2 | async-start | bytes 4194304 | tf_op jit(solution)/shard_map/all_to_all | solution.py:32
  296.3 2.4 copy-start.1
  298.7 1.9 copy-start.9
  321.1 34.5 %all-to-all-start.4 = ((f32[32,16,512]{2,1,0:T(8,128)}), f32[32,16,512]{2,1,0:T(8,128)}, u32[]{:S(2)}, u32[]{:S(2)}) async-start(f32[32,16,512]{2,1,0:T(8,128)} %bitcast.89), calls=%async_computation.4 | async-start | bytes 2097152 | tf_op jit(solution)/shard_map/all_to_all | solution.py:32
  358.8 54.4 %all-to-all-start.3 = ((f32[32,1,16384]{2,1,0:T(1,128)}), f32[32,1,16384]{2,1,0:T(1,128)}, u32[]{:S(2)}, u32[]{:S(2)}) async-start(f32[32,1,16384]{2,1,0:T(1,128)} %broadcast_in_dim.7), calls=%async_computation.3 | async-start | bytes 4194304 | tf_op jit(solution)/shard_map/all_to_all | solution.py:49
  370.9 50.1 %copy-start.11 = (f32[16,1,16384]{2,1,0:T(1,128)S(1)}, f32[16,1,16384]{2,1,0:T(1,128)}, u32[]{:S(2)}) copy-start(f32[16,1,16384]{2,1,0:T(1,128)} %reshape.67) | copy-start | bytes 3145732
  414.3 34.8 %all-to-all-start.5 = ((f32[32,16,512]{2,1,0:T(8,128)}), f32[32,16,512]{2,1,0:T(8,128)}, u32[]{:S(2)}, u32[]{:S(2)}) async-start(f32[32,16,512]{2,1,0:T(8,128)} %broadcast_in_dim.8), calls=%async_computation.5 | async-start | bytes 2097152 | tf_op jit(solution)/shard_map/all_to_all | solution.py:49
  433.1 6.0 %copy-start.2 = (f32[2,512,512]{2,1,0:T(8,128)S(1)}, f32[2,512,512]{2,1,0:T(8,128)}, u32[]{:S(2)}) copy-start(f32[2,512,512]{2,1,0:T(8,128)} %param.12) | copy-start | bytes 6291460
  442.6 1.9 copy-start.12
  442.7 1.9 copy-start.17
  444.6 1.0 copy-start.3
  447.4 1.0 copy-start.10
  449.1 2.8 copy-start.16
  460.1 1.9 copy-start.4
Sparse Core Ops, SparseCore 0:
  9.9 55.2 all-gather.9
  80.0 61.5 all-gather.11
  188.6 48.9 all-gather.15
  239.2 52.4 all-gather.13
where the time goes:
time: 476 us; the launch traced here: 469 us
  waiting for transfers between devices  199 us (42%)
  blocking collectives  108 us (23%)
  matrix products  49.7 us (10%)
  local copies, waits for them, and re-layouts  39.2 us (8%)
  other arithmetic  29.9 us (6%)
  starting transfers between devices  29.6 us (6%)
  between operations  14.4 us (3%)
    all_to_all x1, blocking collectives, shards(): lax.all_to_all(strips, ROW, split_axis=1, concat_axis=0, tiled=True)  63.3 us
    all_gather x2, waiting for transfers between devices, gathered_total(): blocks = lax.all_gather(x, axis)  59 us
    all_gather x1, waiting for transfers between devices, broadcast(): lax.all_gather(x, axis)  55.4 us
    all_to_all x2, waiting for transfers between devices, summed_on_arrival(): blocks = lax.all_to_all(cut_along(x, dim, devices), axis, 0, 0, tiled=True)  43.7 us
    all_to_all x2, waiting for transfers between devices, copy_for_each(): lax.all_to_all(jnp.broadcast_to(x[None], (devices, *x.shape)), axis, 0, 0...  40.9 us
    all_to_all x1, blocking collectives, shards(): lax.all_to_all(lower_half, 'col', split_axis=0, concat_axis=1, tiled=True)  30.5 us
    dot_general x8, matrix products, inner_rows(): lax.dot_general(left_mat, right_mat, (((0,), (0,)), ((), ())), precision=...  21.4 us
    all_to_all x2, starting transfers between devices, summed_on_arrival(): blocks = lax.all_to_all(cut_along(x, dim, devices), axis, 0, 0, tiled=True)  16.9 us
  transfers between devices with their start and end apart: 8, of which 6 were waited for; matrix products, arithmetic and copies ran while one was open for 18% of the time, Pallas kernels for 0%

commit v1 on v0

v1 whole, which is shorter than its diff:
```python
import functools

import jax
import jax.numpy as jnp
from jax import lax
from jax.experimental import pallas as pl
from jax.experimental.pallas import tpu as pltpu
from jax.sharding import Mesh
from jax.sharding import PartitionSpec as P

MESH = pl.DeviceIdType.MESH
F32, BF16 = jnp.float32, jnp.bfloat16
BLOCK = 512
VMEM_BYTES = 56 * 1024 * 1024


def place():
    return tuple(lax.axis_index(a) for a in ("z", "x", "y", "k"))


def meet(peers):
    barrier = pltpu.get_barrier_semaphore()
    for peer in peers:
        pl.semaphore_signal(barrier, inc=1, device_id=peer, device_id_type=MESH)
    pl.semaphore_wait(barrier, len(peers))


def push(src, dst, send, recv, peer):
    return pltpu.make_async_remote_copy(
        src_ref=src, dst_ref=dst, send_sem=send, recv_sem=recv, device_id=peer, device_id_type=MESH
    )


def dot(a, b, ca=1, cb=0):
    return lax.dot_general(a, b, (((ca,), (cb,)), ((), ())), preferred_element_type=F32)


def split(a):
    high = a.astype(BF16)
    return high, (a - high.astype(F32)).astype(BF16)


def dot3(a, b, ca=1, cb=0):
    ah, al = a if isinstance(a, tuple) else split(a)
    bh, bl = b if isinstance(b, tuple) else split(b)
    return dot(ah, bh, ca, cb) + (dot(al, bh, ca, cb) + dot(ah, bl, ca, cb))


def dot2(a, b, ca=1, cb=0):
    if isinstance(a, tuple):
        return dot(a[0], b, ca, cb) + dot(a[1], b, ca, cb)
    return dot(a, b[0], ca, cb) + dot(a, b[1], ca, cb)


def symmetric(f):
    size = f.shape[0]
    rows = lax.broadcasted_iota(jnp.int32, (size, size), 0)
    cols = lax.broadcasted_iota(jnp.int32, (size, size), 1)
    halved = jnp.where(cols < rows, f, jnp.where(cols == rows, f * 0.5, 0.0))
    return halved + halved.T


def exchange_kernel(trail, fac, mx, fz, xs, xr, fs, fr, hs, hr, own_sem):
    z, x, y, k = place()
    c = 2 * y + k
    ys, ks = z >> 1, z & 1
    yn = (lax.rem(y + 3, 4), lax.rem(y + 1, 4))
    xp = [lax.rem(x + d, 4) for d in (1, 2, 3)]
    sibling = (z, x, y, 1 - k)
    meet(
        [(z, p, y, k) for p in xp]
        + [(z, x, yn[s], j) for s in (0, 1) for j in (0, 1)]
        + [sibling]
    )
    lower = c <= z

    def rows(s, i):
        block = lax.rem(x + i // 2, 4)
        return pl.ds(pl.multiple_of(block * BLOCK + s * 256 + (i % 2) * 128, 128), 128)

    def across(d):
        return push(
            trail.at[:, pl.ds(pl.multiple_of(xp[d] * BLOCK, 128), BLOCK)],
            mx.at[pl.ds(pl.multiple_of(x * BLOCK, BLOCK), BLOCK), :],
            xs.at[d],
            xr.at[d],
            (z, xp[d], y, k),
        )

    own_block = pltpu.make_async_copy(
        trail.at[:, pl.ds(pl.multiple_of(x * BLOCK, 128), BLOCK)],
        mx.at[pl.ds(pl.multiple_of(x * BLOCK, BLOCK), BLOCK), :],
        own_sem,
    )
    source_chip = y == ys
    source = source_chip & (k == ks)

    def first_hop(s, i):
        return push(
            fac.at[rows(s, i), :], fz.at[rows(s, i), :], fs.at[s, i], fr.at[i], (z, x, yn[s], s)
        )

    def beside_own(i):
        return push(fac.at[rows(1 - k, i), :], fz.at[rows(1 - k, i), :], hs.at[0, i], fr.at[i], sibling)

    def beside_other(i):
        return push(fac.at[rows(k, i), :], fz.at[rows(k, i), :], hs.at[1, i], hr.at[i], sibling)

    @pl.when(source)
    def _():
        for i in range(8):
            first_hop(0, i).start()
            first_hop(1, i).start()
            beside_own(i).start()
            beside_other(i).start()

    @pl.when(lower)
    def _():
        for d in range(3):
            across(d).start()
        own_block.start()

    onward = jnp.where(k == 0, yn[0], yn[1])
    hops = jnp.where(k == 0, (ys - y + 4) & 3, (y - ys + 4) & 3)

    def forward(i):
        return push(
            fz.at[rows(k, i), :], fz.at[rows(k, i), :], fs.at[0, i], fr.at[i], (z, x, onward, k)
        )

    def share(i):
        return push(fz.at[rows(k, i), :], fz.at[rows(k, i), :], hs.at[0, i], hr.at[i], sibling)

    def other(i):
        return push(fz.at[rows(1 - k, i), :], fz.at[rows(1 - k, i), :], hs.at[0, i], hr.at[i], sibling)

    @pl.when(jnp.logical_not(source_chip))
    def _():
        for i in range(8):
            forward(i).wait_recv()

            @pl.when(hops < 3)
            def _():
                forward(i).start()

            share(i).start()
        for i in range(8):
            other(i).wait_recv()
            share(i).wait_send()

        @pl.when(hops < 3)
        def _():
            for i in range(8):
                forward(i).wait_send()

    @pl.when(source_chip & (k != ks))
    def _():
        for i in range(8):
            forward(i).wait_recv()
            other(i).wait_recv()

    @pl.when(source)
    def _():
        for i in range(8):
            first_hop(0, i).wait_send()
            first_hop(1, i).wait_send()
            beside_own(i).wait_send()
            beside_other(i).wait_send()

    @pl.when(lower)
    def _():
        for d in range(3):
            across(d).wait()
        own_block.wait()


def masked(m, row0, col0):
    rows = row0 + lax.broadcasted_iota(jnp.int32, m.shape, 0)
    cols = col0 + lax.broadcasted_iota(jnp.int32, m.shape, 1)
    scale = jnp.where(cols < rows, 1.0, jnp.where(cols == rows, 0.5, 0.0))
    return (m.astype(F32) * scale).astype(BF16)


def sums_kernel(
    trail, fac, fz, grad, xf, lf, li, cg, dg,
    cross_out, diag_out, mf_out, ph_out, pl_out,
    m, w, full, r0, r1, r2, r3, lit,
    s0, v0, s1, v1, s2, v2, s3, v3, g3, u3, g2, u2, g1, u1, g0, u0,
):
    z, x, y, k = place()
    c = 2 * y + k
    sibling = (z, x, y, 1 - k)
    first = jnp.where(k == 0, y, x)
    second = jnp.where(k == 0, x, y)

    def along_first(p):
        return (z, jnp.where(k == 0, x, p), jnp.where(k == 0, p, y), k)

    def along_second(p):
        return (z, jnp.where(k == 0, p, x), jnp.where(k == 0, y, p), k)

    p1 = [lax.rem(first + d, 4) for d in (1, 2, 3)]
    p2 = [lax.rem(second + d, 4) for d in (1, 2, 3)]
    pz = [lax.rem(z + d, 8) for d in range(1, 8)]
    meet(
        [sibling]
        + [along_first(p) for p in p1]
        + [along_second(p) for p in p2]
        + [(p, x, y, k) for p in pz]
    )

    @pl.when(c <= z)
    def _():
        @pl.loop(0, 4)
        def _(i):
            here = pl.ds(pl.multiple_of(i * 128, 128), 128)
            m[here, :] = trail[here, :]

            @pl.when(c == z)
            def _():
                m[here, :] = masked(trail[here, :], x * BLOCK + i * 128, 0)

            mf_out[here, :] = dot(m[here, :], fac[...])

        mine = pl.ds(pl.multiple_of(x * BLOCK, BLOCK), BLOCK)
        f = jnp.where(c == z, fac[mine, :].astype(F32), fz[mine, :].astype(F32)).astype(BF16)
        own = jnp.where(c == z, 1.0, 0.0)

        def store(block, value):
            for j in range(4):
                w[pl.ds(j * 1536 + block * BLOCK, BLOCK), :] = value[:, j * 128 : (j + 1) * 128]

        for block, (a, b) in enumerate(((1, 1), (1, 0), (0, 0))):
            mfa = mf_out[:, a * BLOCK : (a + 1) * BLOCK]
            mfb = mf_out[:, b * BLOCK : (b + 1) * BLOCK]
            ga = grad[:, a * BLOCK : (a + 1) * BLOCK].astype(F32) * own
            fa = f[:, a * BLOCK : (a + 1) * BLOCK]
            fb = f[:, b * BLOCK : (b + 1) * BLOCK]
            store(block, dot2(split(ga - mfa), fb, 0, 0) - dot2(fa, split(mfb), 0, 0))

    @pl.when(c > z)
    def _():
        mf_out[...] = jnp.zeros_like(mf_out)
        w[...] = jnp.zeros_like(w)

    half = k * 3072

    def part(at, n):
        return pl.ds(pl.multiple_of(at, 8), n)

    c0 = push(w.at[part(3072 - half, 3072), :], r0, s0, v0, sibling)
    c0.start()
    li0, li1 = split(li[0]), split(li[1])
    lf0, lf1, xb = lf[0], lf[1], xf[...]
    j1 = split(dot2(li1, lf1))
    j0 = split(dot2(li0, lf0))
    e1 = dot(lf1, dg[1], 0, 0)
    e0 = dot(lf0, dg[0], 0, 0)
    b1f = dot3(split(dot2(li1, xb)), li0)
    b1 = split(b1f)
    b2 = split(dot2(b1, lf0))
    cj = dot2(cg[...], j0)
    lit[0] = li[0].T
    lit[1] = li[1].T
    ph_out[0:BLOCK, 0:BLOCK], pl_out[0:BLOCK, 0:BLOCK] = li0
    ph_out[BLOCK:, BLOCK:], pl_out[BLOCK:, BLOCK:] = li1
    ph_out[BLOCK:, 0:BLOCK], pl_out[BLOCK:, 0:BLOCK] = -b1[0], -b1[1]
    ph_out[0:BLOCK, BLOCK:] = jnp.zeros((BLOCK, BLOCK), BF16)
    pl_out[0:BLOCK, BLOCK:] = jnp.zeros((BLOCK, BLOCK), BF16)
    c0.wait()
    w[part(half, 3072), :] += r0[...]

    at1 = half + first * 768
    at2 = at1 + second * 192
    at3 = at2 + z * 24

    def out1(d):
        return push(w.at[part(half + p1[d] * 768, 768), :], r1.at[d], s1.at[d], v1.at[d], along_first(p1[d]))

    def out2(d):
        return push(w.at[part(at1 + p2[d] * 192, 192), :], r2.at[d], s2.at[d], v2.at[d], along_second(p2[d]))

    def out3(d):
        return push(w.at[part(at2 + pz[d] * 24, 24), :], r3.at[d], s3.at[d], v3.at[d], (pz[d], x, y, k))

    def whole(at, n, send, recv, peer):
        return push(full.at[part(at, n), :], full.at[part(at, n), :], send, recv, peer)

    def settle(copies):
        for copy in copies:
            copy.start()
        for copy in copies:
            copy.wait()

    settle([out1(d) for d in range(3)])
    w[part(at1, 768), :] += r1[0] + r1[1] + r1[2]
    settle([out2(d) for d in range(3)])
    w[part(at2, 192), :] += r2[0] + r2[1] + r2[2]
    settle([out3(d) for d in range(7)])
    full[part(at3, 24), :] = w[part(at3, 24), :] + ((r3[0] + r3[1]) + (r3[2] + r3[3])) + ((r3[4] + r3[5]) + r3[6])
    settle([whole(at3, 24, g3.at[d], u3.at[d], (pz[d], x, y, k)) for d in range(7)])
    settle([whole(at2, 192, g2.at[d], u2.at[d], along_second(p2[d])) for d in range(3)])
    settle([whole(at1, 768, g1.at[d], u1.at[d], along_first(p1[d])) for d in range(3)])
    settle([whole(half, 3072, g0, u0, sibling)])

    def load(block):
        return split(
            jnp.concatenate([full[pl.ds(j * 1536 + block * BLOCK, BLOCK), :] for j in range(4)], axis=1)
        )

    w11, w10, w00 = load(0), load(1), load(2)
    slab = pl.ds(pl.multiple_of(c * 64, 64), 64)
    lit1, lit0 = split(lit[1, slab, :]), split(lit[0, slab, :])
    sym1 = split(symmetric(e1 - dot3(j1, w11, 0, 0)))
    ls1 = split(dot3(lit1, sym1))
    diag_out[1] = dot3(ls1, li1)
    cross_out[...] = dot2(cg[slab, :], li0) - (dot3(split(dot3(lit1, w10)), li0) + dot3(ls1, b1))
    inner = split(dot3(w10, j0) + dot3(sym1, b2))
    cl = split(cj - dot3(li1, inner, 0, 0))
    g_zero = e0 - dot3(j0, w00, 0, 0) + dot3(b2, w10, 0, 0) - dot2(cl, xb, 0, 0)
    sym0 = split(symmetric(g_zero))
    diag_out[0] = dot3(split(dot3(lit0, sym0)), li0)


CHUNKS = 16
LINES = BLOCK // CHUNKS


def panel_kernel(
    mx, fz, fac, mf, ph, plo, grad, out,
    kept, t, arrived, yp, r0, r1, ts, tr, s0, v0, s1, v1,
):
    z, x, y, k = place()
    c = 2 * y + k
    sibling = (z, x, y, 1 - k)
    py = [lax.rem(y + d, 4) for d in (1, 2, 3)]
    before, after = lax.rem(z + 7, 8), lax.rem(z + 1, 8)
    meet([sibling] + [(z, x, p, k) for p in py] + [(before, x, y, k), (after, x, y, k)])
    lower = c <= z

    @pl.when(c == z)
    def _():
        @pl.loop(0, 16)
        def _(i):
            here = pl.ds(pl.multiple_of(i * 128, 128), 128)
            kept[here, :] = masked(mx[here, :], i * 128, x * BLOCK)

        for i in range(4):
            t[i * 128 : (i + 1) * 128, :] = dot(kept[:, i * 128 : (i + 1) * 128], fac[...], 0, 0)

    @pl.when(c < z)
    def _():
        for i in range(4):
            t[i * 128 : (i + 1) * 128, :] = dot(mx[:, i * 128 : (i + 1) * 128], fz[...], 0, 0)

    @pl.when(jnp.logical_not(lower))
    def _():
        t[...] = jnp.zeros_like(t)

    position = jnp.where(k == 0, 7 - z, (z - c + 7) & 7)
    last = z == c
    taking = (k == 1) | lower
    onward = jnp.where(k == 0, before, after)

    def chunk(i):
        here = pl.ds(i * LINES, LINES)
        return push(t.at[here, :], arrived.at[here, :], ts.at[i], tr.at[i], (onward, x, y, k))

    @pl.when(taking)
    def _():
        for i in range(CHUNKS):
            here = pl.ds(i * LINES, LINES)

            @pl.when(position > 0)
            def _():
                chunk(i).wait_recv()
                t[here, :] += arrived[here, :]

            @pl.when(jnp.logical_not(last))
            def _():
                chunk(i).start()

        @pl.when(jnp.logical_not(last))
        def _():
            for i in range(CHUNKS):
                chunk(i).wait_send()

    chip_lower = 2 * y <= z

    @pl.when(chip_lower)
    def _():
        @pl.loop(0, 4)
        def _(i):
            here = pl.ds(pl.multiple_of(i * 128, 128), 128)
            part = mf[here, :]
            part = jnp.where(last, part + t[here, :], part)
            h, l = split(part)
            for g in range(8):
                cols = slice(g * 128, (g + 1) * 128)
                start = 0 if g < 4 else BLOCK
                yp[g % 2, g // 2, here, :] = dot3(
                    (h[:, start:], l[:, start:]), (ph[start:, cols], plo[start:, cols])
                )

        swap = push(yp.at[1 - k], r0, s0, v0, sibling)
        swap.start()
        swap.wait()
        yp[pl.ds(k, 1)] += r0[...][None]
        for d in range(3):
            push(yp.at[k, py[d]], r1.at[d], s1.at[d], v1.at[d], (z, x, py[d], k)).start()

    cols = pl.ds(pl.multiple_of(c * 128, 128), 128)
    out[...] = dot2(grad[...], (ph[:, cols], plo[:, cols]))

    @pl.when(chip_lower)
    def _():
        out[...] -= yp[k, y]

    for d in range(3):
        came = lax.rem(y + 3 - d, 4)

        @pl.when(2 * came <= z)
        def _():
            push(yp.at[k, py[d]], r1.at[d], s1.at[d], v1.at[d], (z, x, py[d], k)).wait_recv()
            out[...] -= r1[d]

    @pl.when(chip_lower)
    def _():
        for d in range(3):
            push(yp.at[k, py[d]], r1.at[d], s1.at[d], v1.at[d], (z, x, py[d], k)).wait_send()


def params(number):
    return pltpu.CompilerParams(
        collective_id=number, has_side_effects=True, vmem_limit_bytes=VMEM_BYTES
    )


def shards(trail, fac, xf, lf, li, grad, cg, dg):
    dma = pltpu.SemaphoreType.DMA
    anywhere = pl.BlockSpec(memory_space=pl.ANY)
    vmem = pl.BlockSpec(memory_space=pltpu.VMEM)
    shape = jax.ShapeDtypeStruct
    mx, fz = pl.pallas_call(
        exchange_kernel,
        name="exchange",
        out_shape=(shape((2048, BLOCK), BF16), shape((2048, 1024), BF16)),
        in_specs=[anywhere] * 2,
        out_specs=[vmem, anywhere],
        scratch_shapes=[
            dma((3,)), dma((3,)), dma((2, 8)), dma((8,)), dma((2, 8)), dma((8,)), dma,
        ],
        compiler_params=params(0),
    )(trail, fac)
    cross, diag, mf, ph, plo = pl.pallas_call(
        sums_kernel,
        name="sums",
        out_shape=(
            shape((64, BLOCK), F32), shape((2, 64, BLOCK), F32), shape((BLOCK, 1024), F32),
            shape((1024, 1024), BF16), shape((1024, 1024), BF16),
        ),
        in_specs=[vmem] * 9,
        out_specs=[vmem] * 5,
        scratch_shapes=[
            pltpu.VMEM((BLOCK, 2048), BF16),
            pltpu.VMEM((6144, 128), F32),
            pltpu.VMEM((6144, 128), F32),
            pltpu.VMEM((3072, 128), F32),
            pltpu.VMEM((3, 768, 128), F32),
            pltpu.VMEM((3, 192, 128), F32),
            pltpu.VMEM((7, 24, 128), F32),
            pltpu.VMEM((2, BLOCK, BLOCK), F32),
            dma, dma, dma((3,)), dma((3,)), dma((3,)), dma((3,)), dma((7,)), dma((7,)),
            dma((7,)), dma((7,)), dma((3,)), dma((3,)), dma((3,)), dma((3,)), dma, dma,
        ],
        compiler_params=params(1),
    )(trail, fac, fz, grad, xf, lf, li, cg, dg)
    panel = pl.pallas_call(
        panel_kernel,
        name="panel",
        out_shape=shape((BLOCK, 128), F32),
        in_specs=[vmem] * 7,
        out_specs=vmem,
        scratch_shapes=[
            pltpu.VMEM((2048, BLOCK), BF16),
            pltpu.VMEM((BLOCK, 1024), F32),
            pltpu.VMEM((BLOCK, 1024), F32),
            pltpu.VMEM((2, 4, BLOCK, 128), F32),
            pltpu.VMEM((4, BLOCK, 128), F32),
            pltpu.VMEM((3, BLOCK, 128), F32),
            dma((CHUNKS,)), dma((CHUNKS,)), dma, dma, dma((3,)), dma((3,)),
        ],
        compiler_params=params(2),
    )(mx, fz, fac, mf, ph, plo, grad)
    return panel, cross, diag


def solution(mesh):
    fine = Mesh(mesh.devices.reshape(8, 4, 4, 2), ("z", "x", "y", "k"))
    row, col = ("z", "x"), ("y", "k")
    return jax.shard_map(
        shards,
        mesh=fine,
        in_specs=(P(row, col), P(col, None), P(), P(), P(), P(row, None), P(), P()),
        out_specs=(P(row, col), P(col, None), P(None, col, None)),
        check_vma=False,
    )
```

time: 476 us -> 217 us (0.46); the launches traced: 469 us -> 216 us
  Pallas kernels: 0 us -> 213 us
  waiting for transfers between devices: 199 us -> 0 us
  blocking collectives: 108 us -> 0 us
  matrix products: 49.7 us -> 0 us
  local copies, waits for them, and re-layouts: 39.2 us -> 3.04 us
  other arithmetic: 29.9 us -> 0 us
  starting transfers between devices: 29.6 us -> 0 us
  between operations: 14.4 us -> 0.67 us
    pallas_call x0 -> x3, Pallas kernels: none -> 213 us  [the longest x1 102 us: shards(): pl.pallas_call(sums_kernel, name='sums', out_shape=(shape((64, BLOCK), F3...]
    all_gather x4 -> x0, waiting for transfers between devices: 114 us -> none  [the longest x2 59 us: gathered_total(): blocks = lax.all_gather(x, axis)]
    all_to_all x2 -> x0, blocking collectives: 93.9 us -> none  [the longest x1 63.3 us: shards(): lax.all_to_all(strips, ROW, split_axis=1, concat_axis=0, tiled=True)]
    all_to_all x4 -> x0, waiting for transfers between devices: 84.6 us -> none  [the longest x2 43.7 us: summed_on_arrival(): blocks = lax.all_to_all(cut_along(x, dim, devices), axis, 0, 0, tiled=True)]
    dot_general x19 -> x0, matrix products: 49.7 us -> none  [the longest x8 21.4 us: inner_rows(): lax.dot_general(left_mat, right_mat, (((0,), (0,)), ((), ())), precision=...]
    all_to_all x4 -> x0, starting transfers between devices: 29.3 us -> none  [the longest x2 16.9 us: summed_on_arrival(): blocks = lax.all_to_all(cut_along(x, dim, devices), axis, 0, 0, tiled=True)]
    reduce_sum x4 -> x0, other arithmetic: 14.3 us -> none  [the longest x2 9.97 us: gathered_total(): return blocks.sum(axis=0)]
    all_gather x1 -> x0, blocking collectives: 13.8 us -> none  [whole_of(): x = lax.all_gather(x, axis, axis=dim, tiled=True)]
  transfers between devices with their start and end apart: 8 -> 0, of which waited for: 6 -> 0; matrix products, arithmetic and copies ran while one was open for 18% -> 0% of each run, Pallas kernels for 0% -> 0%
where the time goes in v1:
time: 217 us; the launch traced here: 216 us
  Pallas kernels  213 us (98%)
  local copies, waits for them, and re-layouts  3.04 us (1%)
    pallas_call x1, Pallas kernels, shards(): pl.pallas_call(sums_kernel, name='sums', out_shape=(shape((64, BLOCK), F3...  102 us
    pallas_call x1, Pallas kernels, shards(): pl.pallas_call(panel_kernel, name='panel', out_shape=shape((BLOCK, 128),...  81.5 us
    pallas_call x1, Pallas kernels, shards(): pl.pallas_call(exchange_kernel, name='exchange', out_shape=(shape((2048,...  28.9 us

profile of v1, /device:TPU:2, one launch (start us, length us, event | category | flops | bytes accessed | tf_op | source)
XLA Modules:
  0.0 216.5 jit_solution(3907483868460321644)
XLA Ops:
  0.6 28.9 %exchange.1 = (bf16[2048,512]{1,0:T(8,128)(2,1)}, bf16[2048,1024]{1,0:T(8,128)(2,1)}) custom-call(bf16[512,2048]{1,0:T(8,128)(2,1)} %trail.3, bf16[2048,1024]{1,0:T(8,128)(2,1)} %fac.5), custom_call_target="tpu_custom_call" | custom-call | tf_op jit(solution)/shard_map/exchange/pallas_call | solution.py:444
  29.5 102.4 %sums.1 = (f32[64,512]{1,0:T(8,128)}, f32[2,64,512]{2,1,0:T(8,128)}, f32[512,1024]{1,0:T(8,128)}, bf16[1024,1024]{1,0:T(8,128)(2,1)}, bf16[1024,1024]{1,0:T(8,128)(2,1)}) custom-call(bf16[512,2048]{1,0:T(8,128)(2,1)} %trail.3, bf16[2048,1024]{1,0:T(8,128)(2,1)} %fac.5, bf16[2048,1024]{1,0:T(8,128)(2,1)} %get-tuple-element.11.fz, bf16[512,1024]{1,0:T(8,128)(2,1)} %grad.3, ...), custom_call_target="tpu_custom_call" | custom-call | tf_op jit(solution)/shard_map/sums/pallas_call | solution.py:455
  132.0 0.0 copy-start.1
  132.0 0.0 copy-start
  132.0 81.5 %panel.1 = f32[512,128]{1,0:T(8,128)} custom-call(bf16[2048,512]{1,0:T(8,128)(2,1)} %get-tuple-element.10.mx, bf16[2048,1024]{1,0:T(8,128)(2,1)} %get-tuple-element.11.fz, bf16[2048,1024]{1,0:T(8,128)(2,1)} %fac.5, f32[512,1024]{1,0:T(8,128)} %get-tuple-element.12.mf, bf16[1024,1024]{1,0:T(8,128)(2,1)} %get-tuple-element.13.ph, ...), custom_call_target="tpu_custom_call" | custom-call | tf_op jit(solution)/shard_map/panel/pallas_call | solution.py:478
  213.4 1.7 copy.14
  215.1 0.0 copy-done.1
  215.1 0.7 copy.15
  215.8 0.0 copy-done
  215.8 0.7 copy.16
Async XLA Ops:
  132.0 83.2 %copy-start.1 = (f32[64,512]{1,0:T(8,128)S(1)}, f32[64,512]{1,0:T(8,128)}, u32[]{:S(2)}) copy-start(f32[64,512]{1,0:T(8,128)} %get-tuple-element.21) | copy-start | bytes 393220
  132.0 83.8 %copy-start = (f32[2,64,512]{2,1,0:T(8,128)S(1)}, f32[2,64,512]{2,1,0:T(8,128)}, u32[]{:S(2)}) copy-start(f32[2,64,512]{2,1,0:T(8,128)} %get-tuple-element.22) | copy-start | bytes 786436

commit v2 on v0

v2 whole, which is shorter than its diff:
```python
import jax
import jax.numpy as jnp
from jax import lax
from jax.experimental import pallas as pl
from jax.experimental.pallas import tpu as pltpu
from jax.sharding import Mesh
from jax.sharding import PartitionSpec as P

MESH = pl.DeviceIdType.MESH
F32, BF16 = jnp.float32, jnp.bfloat16
BLOCK = 512
VMEM_BYTES = 62 * 1024 * 1024


def place():
    return tuple(lax.axis_index(a) for a in ("z", "x", "y", "k"))


def meet(peers):
    barrier = pltpu.get_barrier_semaphore()
    for peer in peers:
        pl.semaphore_signal(barrier, inc=1, device_id=peer, device_id_type=MESH)
    pl.semaphore_wait(barrier, len(peers))


def push(src, dst, send, recv, peer):
    return pltpu.make_async_remote_copy(
        src_ref=src, dst_ref=dst, send_sem=send, recv_sem=recv, device_id=peer, device_id_type=MESH
    )


def dot(a, b, ca=1, cb=0):
    return lax.dot_general(a, b, (((ca,), (cb,)), ((), ())), preferred_element_type=F32)


def split(a):
    high = a.astype(BF16)
    return high, (a - high.astype(F32)).astype(BF16)


def dot3(a, b, ca=1, cb=0):
    ah, al = a if isinstance(a, tuple) else split(a)
    bh, bl = b if isinstance(b, tuple) else split(b)
    return dot(ah, bh, ca, cb) + (dot(al, bh, ca, cb) + dot(ah, bl, ca, cb))


def dot2(a, b, ca=1, cb=0):
    if isinstance(a, tuple):
        return dot(a[0], b, ca, cb) + dot(a[1], b, ca, cb)
    return dot(a, b[0], ca, cb) + dot(a, b[1], ca, cb)


def symmetric(f):
    size = f.shape[0]
    rows = lax.broadcasted_iota(jnp.int32, (size, size), 0)
    cols = lax.broadcasted_iota(jnp.int32, (size, size), 1)
    halved = jnp.where(cols < rows, f, jnp.where(cols == rows, f * 0.5, 0.0))
    return halved + halved.T


def masked(m, row0, col0):
    rows = row0 + lax.broadcasted_iota(jnp.int32, m.shape, 0)
    cols = col0 + lax.broadcasted_iota(jnp.int32, m.shape, 1)
    scale = jnp.where(cols < rows, 1.0, jnp.where(cols == rows, 0.5, 0.0))
    return (m.astype(F32) * scale).astype(BF16)

CHUNKS = 16
LINES = BLOCK // CHUNKS
HOPS = 16


def kernel(
    trail, fac, xf, lf, li, grad, cg, dg,
    panel_out, cross_out, diag_out,
    m, fv, gv, xv, lfv, liv, cgv, dgv,
    mx, fz, f, mf, t, arrived, w, full, r1, r2, r3,
    ph, plo, pairs, consts, yp, q0, q1, tq, rt,
    ls, fs, fr, hs, hr, xs, xr,
    s0, v0, s1, v1, s2, v2, s3, v3, g3, u3, g2, u2, g1, u1, g0, u0,
    ts, tr, a0, b0, a1, b1s, es, er,
):
    z, x, y, k = place()
    c = 2 * y + k
    ys, ks = z >> 1, z & 1
    sibling = (z, x, y, 1 - k)
    lower = c <= z
    last = c == z
    chip_lower = 2 * y <= z
    source_chip = y == ys
    yn = (lax.rem(y + 3, 4), lax.rem(y + 1, 4))
    px = [lax.rem(x + d, 4) for d in (1, 2, 3)]
    py = [lax.rem(y + d, 4) for d in (1, 2, 3)]
    pz = [lax.rem(z + d, 8) for d in range(1, 8)]
    pc = [lax.rem(c + d, 8) for d in range(1, 8)]
    mine = pl.ds(pl.multiple_of(x * BLOCK, BLOCK), BLOCK)

    def local(n, src, dst):
        return pltpu.make_async_copy(src, dst, ls.at[n])

    get_trail = local(0, trail, m)
    get_factor = local(1, fac, fv)
    get_grad = local(2, grad, gv)
    get_small = [
        local(3, xf, xv), local(4, lf, lfv), local(5, li, liv), local(6, cg, cgv), local(7, dg, dgv)
    ]
    get_own = local(8, trail.at[:, mine], mx.at[mine, :])
    get_source = local(9, fac, fz)

    @pl.when(lower)
    def _():
        get_trail.start()
        get_factor.start()
        get_own.start()

    get_grad.start()
    for copy in get_small:
        copy.start()

    @pl.when(last)
    def _():
        get_source.start()

    meet(
        [(z, p, y, k) for p in px]
        + [(z, x, p >> 1, p & 1) for p in pc]
        + [(p, x, y, k) for p in pz]
    )

    def rows(s, i):
        block = lax.rem(x + i // 4, 4)
        return pl.ds(pl.multiple_of(block * BLOCK + s * 256 + lax.rem(i, 4) * 64, 64), 64)

    def first_hop(s, i):
        return push(
            fac.at[rows(s, i), :], fz.at[rows(s, i), :], fs.at[s, i], fr.at[i], (z, x, yn[s], s)
        )

    def beside_own(i):
        return push(fac.at[rows(1 - k, i), :], fz.at[rows(1 - k, i), :], hs.at[0, i], fr.at[i], sibling)

    def beside_other(i):
        return push(fac.at[rows(k, i), :], fz.at[rows(k, i), :], hs.at[1, i], hr.at[i], sibling)

    onward_y = jnp.where(k == 0, yn[0], yn[1])
    hops = jnp.where(k == 0, (ys - y + 4) & 3, (y - ys + 4) & 3)

    def forward(i):
        return push(
            fz.at[rows(k, i), :], fz.at[rows(k, i), :], fs.at[0, i], fr.at[i], (z, x, onward_y, k)
        )

    def share(i):
        return push(fz.at[rows(k, i), :], fz.at[rows(k, i), :], hs.at[0, i], hr.at[i], sibling)

    def other(i):
        return push(fz.at[rows(1 - k, i), :], fz.at[rows(1 - k, i), :], hs.at[0, i], hr.at[i], sibling)

    def across(d):
        return push(
            trail.at[:, pl.ds(pl.multiple_of(px[d] * BLOCK, 128), BLOCK)],
            mx.at[mine, :],
            xs.at[d],
            xr.at[d],
            (z, px[d], y, k),
        )

    @pl.when(last)
    def _():
        @pl.loop(0, HOPS)
        def _(i):
            first_hop(0, i).start()
            first_hop(1, i).start()
            beside_own(i).start()
            beside_other(i).start()

    @pl.when(lower)
    def _():
        for d in (2, 1, 0):
            across(d).start()

    def relays(lo, hi):
        @pl.when(jnp.logical_not(source_chip))
        def _():
            @pl.loop(lo, hi)
            def _(i):
                forward(i).wait_recv()

                @pl.when(hops < 3)
                def _():
                    forward(i).start()

                share(i).start()

        @pl.when(source_chip & (k != ks))
        def _():
            @pl.loop(lo, hi)
            def _(i):
                forward(i).wait_recv()

    def others(lo, hi):
        @pl.when(jnp.logical_not(last))
        def _():
            @pl.loop(lo, hi)
            def _(i):
                other(i).wait_recv()

    @pl.when(lower)
    def _():
        get_trail.wait()
        get_factor.wait()

        @pl.loop(0, 4)
        def _(i):
            here = pl.ds(pl.multiple_of(i * 128, 128), 128)

            @pl.when(last)
            def _():
                m[here, :] = masked(m[here, :], x * BLOCK + i * 128, 0)

            mf[here, :] = dot(m[here, :], fv[...])

    @pl.when(c > z)
    def _():
        mf[...] = jnp.zeros_like(mf)
        w[...] = jnp.zeros_like(w)
        t[...] = jnp.zeros_like(t)

    get_grad.wait()

    @pl.when(last)
    def _():
        get_source.wait()

    relays(0, 4)
    others(0, 4)

    @pl.when(lower)
    def _():
        f[...] = fz[mine, :]

    own = jnp.where(last, 1.0, 0.0)

    def add_block(block, a, b):
        @pl.when(lower)
        def _():
            mfa = mf[:, a * BLOCK : (a + 1) * BLOCK]
            mfb = mf[:, b * BLOCK : (b + 1) * BLOCK]
            ga = gv[:, a * BLOCK : (a + 1) * BLOCK].astype(F32) * own
            fa = f[:, a * BLOCK : (a + 1) * BLOCK]
            fb = f[:, b * BLOCK : (b + 1) * BLOCK]
            value = dot2(split(ga - mfa), fb, 0, 0) - dot2(fa, split(mfb), 0, 0)
            for j in range(4):
                w[pl.ds(j * 1536 + block * BLOCK, BLOCK), :] = value[:, j * 128 : (j + 1) * 128]

    add_block(0, 1, 1)
    relays(4, 6)
    add_block(1, 1, 0)
    relays(6, 8)
    add_block(2, 0, 0)

    half = k * 3072
    first = jnp.where(k == 0, y, x)
    second = jnp.where(k == 0, x, y)
    p1 = [lax.rem(first + d, 4) for d in (1, 2, 3)]
    p2 = [lax.rem(second + d, 4) for d in (1, 2, 3)]
    at1 = half + first * 768
    at2 = at1 + second * 192
    at3 = at2 + z * 24

    def part(at, n):
        return pl.ds(pl.multiple_of(at, 8), n)

    def along_first(p):
        return (z, jnp.where(k == 0, x, p), jnp.where(k == 0, p, y), k)

    def along_second(p):
        return (z, jnp.where(k == 0, p, x), jnp.where(k == 0, y, p), k)

    def out1(d):
        return push(w.at[part(half + p1[d] * 768, 768), :], r1.at[d], s1.at[d], v1.at[d], along_first(p1[d]))

    def out2(d):
        return push(w.at[part(at1 + p2[d] * 192, 192), :], r2.at[d], s2.at[d], v2.at[d], along_second(p2[d]))

    def out3(d):
        return push(w.at[part(at2 + pz[d] * 24, 24), :], r3.at[d], s3.at[d], v3.at[d], (pz[d], x, y, k))

    def whole(at, n, send, recv, peer):
        return push(full.at[part(at, n), :], full.at[part(at, n), :], send, recv, peer)

    def start(copies):
        for copy in copies:
            copy.start()

    def finish(copies):
        for copy in copies:
            copy.wait()

    other_half = part(3072 - half, 3072)
    c0 = [push(w.at[other_half, :], full.at[other_half, :], s0, v0, sibling)]
    c1 = [out1(d) for d in range(3)]
    c2 = [out2(d) for d in range(3)]
    c3 = [out3(d) for d in range(7)]
    c4 = [whole(at3, 24, g3.at[d], u3.at[d], (pz[d], x, y, k)) for d in range(7)]
    c5 = [whole(at2, 192, g2.at[d], u2.at[d], along_second(p2[d])) for d in range(3)]
    c6 = [whole(at1, 768, g1.at[d], u1.at[d], along_first(p1[d])) for d in range(3)]
    c7 = [whole(half, 3072, g0, u0, sibling)]
    start(c0)

    def pre_one():
        finish(get_small)
        li0, li1 = split(liv[0]), split(liv[1])
        ph[0:BLOCK, 0:BLOCK], plo[0:BLOCK, 0:BLOCK] = li0
        ph[BLOCK:, BLOCK:], plo[BLOCK:, BLOCK:] = li1
        ph[0:BLOCK, BLOCK:] = jnp.zeros((BLOCK, BLOCK), BF16)
        plo[0:BLOCK, BLOCK:] = jnp.zeros((BLOCK, BLOCK), BF16)
        high, low = split(dot3(split(dot2(li1, xv[...])), li0))
        ph[BLOCK:, 0:BLOCK], plo[BLOCK:, 0:BLOCK] = -high, -low

    def li0():
        return ph[0:BLOCK, 0:BLOCK], plo[0:BLOCK, 0:BLOCK]

    def li1():
        return ph[BLOCK:, BLOCK:], plo[BLOCK:, BLOCK:]

    def minus_b1():
        return ph[BLOCK:, 0:BLOCK], plo[BLOCK:, 0:BLOCK]

    def pair(n):
        return pairs[2 * n], pairs[2 * n + 1]

    def keep(n, value):
        pairs[2 * n], pairs[2 * n + 1] = split(value)

    def pre_two():
        keep(0, dot2(li0(), lfv[0]))
        keep(1, dot2(li1(), lfv[1]))
        keep(2, -dot2(minus_b1(), lfv[0]))

    def pre_three():
        consts[0] = dot(lfv[0], dgv[0], 0, 0)
        consts[1] = dot(lfv[1], dgv[1], 0, 0)
        consts[2] = dot2(cgv[...], pair(0))

    def transposed(j):
        @pl.when(lower)
        def _():
            if j == 0:
                get_own.wait()
            else:
                across(3 - j).wait_recv()
            block = lax.rem(x + j, 4)
            here = pl.ds(pl.multiple_of(block * BLOCK, BLOCK), BLOCK)

            @pl.when(last)
            def _():
                mx[here, :] = masked(mx[here, :], block * BLOCK, x * BLOCK)

            @pl.loop(0, 4)
            def _(i):
                lines = pl.ds(pl.multiple_of(i * 128, 128), 128)
                value = dot(mx[here, lines], fz[here, :], 0, 0)
                if j == 0:
                    t[lines, :] = value
                else:
                    t[lines, :] += value

    pre_one()
    relays(8, 9)
    transposed(0)
    relays(9, 10)
    pre_two()
    relays(10, 11)
    finish(c0)
    w[part(half, 3072), :] += full[part(half, 3072), :]
    start(c1)
    relays(11, 12)
    others(4, 8)
    transposed(1)
    relays(12, 14)
    others(8, 12)
    transposed(2)
    relays(14, 16)
    others(12, 16)
    transposed(3)

    before, after = lax.rem(z + 7, 8), lax.rem(z + 1, 8)
    position = jnp.where(k == 0, 7 - z, (z - c + 7) & 7)
    taking = (k == 1) | lower
    onward_z = jnp.where(k == 0, before, after)

    def chunk(i):
        here = pl.ds(i * LINES, LINES)
        return push(t.at[here, :], arrived.at[here, :], ts.at[i], tr.at[i], (onward_z, x, y, k))

    def chain(i):
        here = pl.ds(i * LINES, LINES)

        @pl.when(taking)
        def _():
            @pl.when(position > 0)
            def _():
                chunk(i).wait_recv()
                t[here, :] += arrived[here, :]

            @pl.when(jnp.logical_not(last))
            def _():
                chunk(i).start()

    def mapped(part_rows, store):
        h, l = split(part_rows)
        for g in range(8):
            cols = slice(g * 128, (g + 1) * 128)
            at = 0 if g < 4 else BLOCK
            store(g, dot3((h[:, at:], l[:, at:]), (ph[at:, cols], plo[at:, cols])))

    def direct(i):
        @pl.when(chip_lower)
        def _():
            here = slice(i * 128, (i + 1) * 128)

            def store(g, value):
                yp[g % 2, g // 2, here, :] = value

            mapped(mf[here, :], store)

    swap = push(yp.at[1 - k], q0, a0, b0, sibling)

    def spread(d):
        return push(yp.at[k, py[d]], q1.at[d], a1.at[d], b1s.at[d], (z, x, py[d], k))

    def swap_start():
        @pl.when(chip_lower)
        def _():
            swap.start()

    def swap_end():
        @pl.when(chip_lower)
        def _():
            swap.wait()
            yp[pl.ds(k, 1)] += q0[...][None]
            for d in range(3):
                spread(d).start()

    def scatter(d, i):
        here = pl.ds(i * 128, 128)
        to = pc[d]
        return push(tq.at[to, here, :], rt.at[here, :], es.at[d, i], er.at[i], (z, x, to >> 1, to & 1))

    def last_part(i):
        @pl.when(last)
        def _():
            here = slice(i * 128, (i + 1) * 128)

            def store(g, value):
                tq[g, here, :] = value

            mapped(t[here, :], store)
            for d in range(7):
                scatter(d, i).start()

    def sum_one():
        finish(c1)
        w[part(at1, 768), :] += r1[0] + r1[1] + r1[2]
        start(c2)

    def sum_two():
        finish(c2)
        w[part(at2, 192), :] += r2[0] + r2[1] + r2[2]
        start(c3)

    def sum_three():
        finish(c3)
        full[part(at3, 24), :] = w[part(at3, 24), :] + (
            ((r3[0] + r3[1]) + (r3[2] + r3[3])) + ((r3[4] + r3[5]) + r3[6])
        )
        start(c4)

    def then(done, go):
        def run():
            finish(done)
            start(go)

        return run

    beside = {
        0: [sum_one],
        1: [lambda: direct(0)],
        2: [sum_two],
        3: [lambda: direct(1)],
        4: [sum_three],
        5: [lambda: direct(2)],
        6: [then(c4, c5)],
        7: [lambda: direct(3), swap_start],
        8: [then(c5, c6)],
        9: [swap_end],
        10: [pre_three],
        11: [then(c6, c7)],
    }
    for i in range(CHUNKS):
        chain(i)
        if i % 4 == 3:
            last_part(i // 4)
        for step in beside.get(i, []):
            step()

    finish(c7)

    def load(block):
        return split(
            jnp.concatenate([full[pl.ds(j * 1536 + block * BLOCK, BLOCK), :] for j in range(4)], axis=1)
        )

    w11, w10, w00 = load(0), load(1), load(2)
    slab = pl.ds(pl.multiple_of(c * 64, 64), 64)
    pick = jnp.where(
        lax.broadcasted_iota(jnp.int32, (BLOCK, 64), 0)
        == c * 64 + lax.broadcasted_iota(jnp.int32, (BLOCK, 64), 1),
        1.0,
        0.0,
    ).astype(BF16)

    def turned(parts):
        return tuple(dot(pick, part_of, 0, 1).astype(BF16) for part_of in parts)

    lit1, lit0 = turned(li1()), turned(li0())
    sym1 = split(symmetric(consts[1] - dot3(pair(1), w11, 0, 0)))
    inner = split(dot3(w10, pair(0)) + dot3(sym1, pair(2)))
    cl = split(consts[2] - dot3(li1(), inner, 0, 0))
    g_zero = consts[0] - dot3(pair(0), w00, 0, 0) + dot3(pair(2), w10, 0, 0) - dot2(cl, xv[...], 0, 0)
    sym0 = split(symmetric(g_zero))
    ls1 = split(dot3(lit1, sym1))
    diag_out[1] = dot3(ls1, li1())
    cross_out[...] = dot2(cgv[slab, :], li0()) - (
        dot3(split(dot3(lit1, w10)), li0()) - dot3(ls1, minus_b1())
    )
    diag_out[0] = dot3(split(dot3(lit0, sym0)), li0())

    cols = pl.ds(pl.multiple_of(c * 128, 128), 128)
    panel_out[...] = dot2(gv[...], (ph[:, cols], plo[:, cols]))

    @pl.when(chip_lower)
    def _():
        panel_out[...] -= yp[k, y]

    for d in range(3):
        @pl.when(2 * lax.rem(y + 3 - d, 4) <= z)
        def _():
            spread(d).wait_recv()
            panel_out[...] -= q1[d]

    @pl.when(last)
    def _():
        panel_out[...] -= tq[c]

    @pl.when(jnp.logical_not(last))
    def _():
        for i in range(4):
            scatter(0, i).wait_recv()
        panel_out[...] -= rt[...]

    @pl.when(last)
    def _():
        @pl.loop(0, HOPS)
        def _(i):
            first_hop(0, i).wait_send()
            first_hop(1, i).wait_send()
            beside_own(i).wait_send()
            beside_other(i).wait_send()

        for i in range(4):
            for d in range(7):
                scatter(d, i).wait_send()

    @pl.when(jnp.logical_not(source_chip))
    def _():
        @pl.loop(0, HOPS)
        def _(i):
            share(i).wait_send()

            @pl.when(hops < 3)
            def _():
                forward(i).wait_send()

    @pl.when(lower)
    def _():
        for d in range(3):
            across(d).wait_send()

    @pl.when(taking & jnp.logical_not(last))
    def _():
        for i in range(CHUNKS):
            chunk(i).wait_send()

    @pl.when(chip_lower)
    def _():
        for d in range(3):
            spread(d).wait_send()


def shards(trail, fac, xf, lf, li, grad, cg, dg):
    dma = pltpu.SemaphoreType.DMA
    anywhere = pl.BlockSpec(memory_space=pl.ANY)
    vmem = pl.BlockSpec(memory_space=pltpu.VMEM)
    shape = jax.ShapeDtypeStruct
    square = (BLOCK, BLOCK)
    return pl.pallas_call(
        kernel,
        name="adjoint",
        out_shape=(
            shape((BLOCK, 128), F32), shape((64, BLOCK), F32), shape((2, 64, BLOCK), F32),
        ),
        in_specs=[anywhere] * 8,
        out_specs=[vmem] * 3,
        scratch_shapes=[
            pltpu.VMEM((BLOCK, 2048), BF16),
            pltpu.VMEM((2048, 1024), BF16),
            pltpu.VMEM((BLOCK, 1024), BF16),
            pltpu.VMEM(square, BF16),
            pltpu.VMEM((2, *square), BF16),
            pltpu.VMEM((2, *square), F32),
            pltpu.VMEM(square, BF16),
            pltpu.VMEM((2, *square), BF16),
            pltpu.VMEM((2048, BLOCK), BF16),
            pltpu.VMEM((2048, 1024), BF16),
            pltpu.VMEM((BLOCK, 1024), BF16),
            pltpu.VMEM((BLOCK, 1024), F32),
            pltpu.VMEM((BLOCK, 1024), F32),
            pltpu.VMEM((BLOCK, 1024), F32),
            pltpu.VMEM((6144, 128), F32),
            pltpu.VMEM((6144, 128), F32),
            pltpu.VMEM((3, 768, 128), F32),
            pltpu.VMEM((3, 192, 128), F32),
            pltpu.VMEM((7, 24, 128), F32),
            pltpu.VMEM((1024, 1024), BF16),
            pltpu.VMEM((1024, 1024), BF16),
            pltpu.VMEM((6, *square), BF16),
            pltpu.VMEM((3, *square), F32),
            pltpu.VMEM((2, 4, BLOCK, 128), F32),
            pltpu.VMEM((4, BLOCK, 128), F32),
            pltpu.VMEM((3, BLOCK, 128), F32),
            pltpu.VMEM((8, BLOCK, 128), F32),
            pltpu.VMEM((BLOCK, 128), F32),
            dma((10,)), dma((2, HOPS)), dma((HOPS,)), dma((2, HOPS)), dma((HOPS,)), dma((3,)), dma((3,)),
            dma, dma, dma((3,)), dma((3,)), dma((3,)), dma((3,)), dma((7,)), dma((7,)),
            dma((7,)), dma((7,)), dma((3,)), dma((3,)), dma((3,)), dma((3,)), dma, dma,
            dma((CHUNKS,)), dma((CHUNKS,)), dma, dma, dma((3,)), dma((3,)), dma((7, 4)), dma((4,)),
        ],
        compiler_params=pltpu.CompilerParams(
            collective_id=0, has_side_effects=True, vmem_limit_bytes=VMEM_BYTES
        ),
    )(trail, fac, xf, lf, li, grad, cg, dg)


def solution(mesh):
    fine = Mesh(mesh.devices.reshape(8, 4, 4, 2), ("z", "x", "y", "k"))
    row, col = ("z", "x"), ("y", "k")
    return jax.shard_map(
        shards,
        mesh=fine,
        in_specs=(P(row, col), P(col, None), P(), P(), P(), P(row, None), P(), P()),
        out_specs=(P(row, col), P(col, None), P(None, col, None)),
        check_vma=False,
    )
```

time: 476 us -> 204 us (0.43)
  waiting for transfers between devices: 199 us -> 0 us
  Pallas kernels: 0 us -> 196 us
  blocking collectives: 108 us -> 0 us
  matrix products: 49.7 us -> 0 us
  local copies, waits for them, and re-layouts: 39.2 us -> 4.91 us
  other arithmetic: 29.9 us -> 0 us
  starting transfers between devices: 29.6 us -> 0 us
  between operations: 14.4 us -> 0.64 us
    pallas_call x0 -> x1, Pallas kernels: none -> 196 us  [shards(): pl.pallas_call(kernel, name='adjoint', out_shape=(shape((BLOCK, 128), F32...]
    all_gather x4 -> x0, waiting for transfers between devices: 114 us -> none  [the longest x2 59 us: gathered_total(): blocks = lax.all_gather(x, axis)]
    all_to_all x2 -> x0, blocking collectives: 93.9 us -> none  [the longest x1 63.3 us: shards(): lax.all_to_all(strips, ROW, split_axis=1, concat_axis=0, tiled=True)]
    all_to_all x4 -> x0, waiting for transfers between devices: 84.6 us -> none  [the longest x2 43.7 us: summed_on_arrival(): blocks = lax.all_to_all(cut_along(x, dim, devices), axis, 0, 0, tiled=True)]
    dot_general x19 -> x0, matrix products: 49.7 us -> none  [the longest x8 21.4 us: inner_rows(): lax.dot_general(left_mat, right_mat, (((0,), (0,)), ((), ())), precision=...]
    all_to_all x4 -> x0, starting transfers between devices: 29.3 us -> none  [the longest x2 16.9 us: summed_on_arrival(): blocks = lax.all_to_all(cut_along(x, dim, devices), axis, 0, 0, tiled=True)]
    reduce_sum x4 -> x0, other arithmetic: 14.3 us -> none  [the longest x2 9.97 us: gathered_total(): return blocks.sum(axis=0)]
    all_gather x1 -> x0, blocking collectives: 13.8 us -> none  [whole_of(): x = lax.all_gather(x, axis, axis=dim, tiled=True)]
  transfers between devices with their start and end apart: 8 -> 0, of which waited for: 6 -> 0; matrix products, arithmetic and copies ran while one was open for 18% -> 0% of each run, Pallas kernels for 0% -> 0%
where the time goes in v2:
time: 204 us; the launch traced here: 201 us
  Pallas kernels  196 us (96%)
  local copies, waits for them, and re-layouts  4.91 us (2%)
    pallas_call x1, Pallas kernels, shards(): pl.pallas_call(kernel, name='adjoint', out_shape=(shape((BLOCK, 128), F32...  196 us
    unnamed x3, local copies, waits for them, and re-layouts  4.91 us

profile of v2, /device:TPU:2, one launch (start us, length us, event | category | flops | bytes accessed | tf_op | source)
XLA Modules:
  0.0 201.5 jit_solution(11919393154306935150)
XLA Ops:
  0.6 195.9 %adjoint.1 = (f32[512,128]{1,0:T(8,128)}, f32[64,512]{1,0:T(8,128)}, f32[2,64,512]{2,1,0:T(8,128)}) custom-call(bf16[512,2048]{1,0:T(8,128)(2,1)} %trail.1, bf16[2048,1024]{1,0:T(8,128)(2,1)} %fac.1, bf16[512,512]{1,0:T(8,128)(2,1)} %xf.1, bf16[2,512,512]{2,1,0:T(8,128)(2,1)} %lf.1, f32[2,512,512]{2,1,0:T(8,128)} %li.1, bf16[512,1024]{1,0:T(8,128)(2,1)} %grad.1, ...), custom_call_target="tpu_custom_call" | custom-call | tf_op jit(solution)/shard_map/adjoint/pallas_call | solution.py:607
  196.6 1.7 copy.14
  198.2 1.6 copy.15
  199.8 1.7 copy.16

commit v3 on v2

--- a/solution.py
+++ b/solution.py
@@ -164,14 +164,22 @@
             (z, px[d], y, k),
         )
 
-    @pl.when(last)
-    def _():
-        @pl.loop(0, HOPS)
-        def _(i):
-            first_hop(0, i).start()
-            first_hop(1, i).start()
-            beside_own(i).start()
-            beside_other(i).start()
+    def feed(lo, hi):
+        @pl.when(last)
+        def _():
+            @pl.loop(lo, min(hi, HOPS))
+            def _(i):
+                @pl.when(i >= 2)
+                def _():
+                    first_hop(0, i - 2).wait_send()
+                    first_hop(1, i - 2).wait_send()
+
+                first_hop(0, i).start()
+                first_hop(1, i).start()
+                beside_own(i).start()
+                beside_other(i).start()
+
+    feed(0, 2)
 
     @pl.when(lower)
     def _():
@@ -179,6 +187,8 @@
             across(d).start()
 
     def relays(lo, hi):
+        feed(lo + 2, hi + 2)
+
         @pl.when(jnp.logical_not(source_chip))
         def _():
             @pl.loop(lo, hi)
@@ -296,15 +306,23 @@
         for copy in copies:
             copy.wait()
 
-    other_half = part(3072 - half, 3072)
-    c0 = [push(w.at[other_half, :], full.at[other_half, :], s0, v0, sibling)]
+    def quarter(at, j):
+        return part(at + lax.rem(j, 4) * 768, 768)
+
+    def swapped(j):
+        away = quarter(3072 - half, second + 1 + j)
+        return push(w.at[away, :], full.at[away, :], s0.at[j], v0.at[j], sibling)
+
+    c0 = [swapped(j) for j in range(4)]
     c1 = [out1(d) for d in range(3)]
     c2 = [out2(d) for d in range(3)]
     c3 = [out3(d) for d in range(7)]
     c4 = [whole(at3, 24, g3.at[d], u3.at[d], (pz[d], x, y, k)) for d in range(7)]
     c5 = [whole(at2, 192, g2.at[d], u2.at[d], along_second(p2[d])) for d in range(3)]
     c6 = [whole(at1, 768, g1.at[d], u1.at[d], along_first(p1[d])) for d in range(3)]
-    c7 = [whole(half, 3072, g0, u0, sibling)]
+    c7 = [
+        whole(half + lax.rem(first + 4 - j, 4) * 768, 768, g0.at[j], u0.at[j], sibling) for j in range(4)
+    ]
     start(c0)
 
     def pre_one():
@@ -356,9 +374,9 @@
             def _():
                 mx[here, :] = masked(mx[here, :], block * BLOCK, x * BLOCK)
 
-            @pl.loop(0, 4)
+            @pl.loop(0, 2)
             def _(i):
-                lines = pl.ds(pl.multiple_of(i * 128, 128), 128)
+                lines = pl.ds(pl.multiple_of(i * 256, 256), 256)
                 value = dot(mx[here, lines], fz[here, :], 0, 0)
                 if j == 0:
                     t[lines, :] = value
@@ -371,9 +389,12 @@
     relays(9, 10)
     pre_two()
     relays(10, 11)
-    finish(c0)
-    w[part(half, 3072), :] += full[part(half, 3072), :]
-    start(c1)
+    for j in range(4):
+        c0[j].wait_recv()
+        here = quarter(half, first + 1 + j)
+        w[here, :] += full[here, :]
+        if j < 3:
+            c1[j].start()
     relays(11, 12)
     others(4, 8)
     transposed(1)
@@ -390,14 +411,67 @@
     onward_z = jnp.where(k == 0, before, after)
 
     def chunk(i):
-        here = pl.ds(i * LINES, LINES)
+        here = pl.ds(pl.multiple_of(i * LINES, LINES), LINES)
         return push(t.at[here, :], arrived.at[here, :], ts.at[i], tr.at[i], (onward_z, x, y, k))
 
-    def chain(i):
-        here = pl.ds(i * LINES, LINES)
-
-        @pl.when(taking)
-        def _():
+    def mapped(part_rows, store):
+        h, l = split(part_rows)
+        low = dot3((h, l), (ph[:, :BLOCK], plo[:, :BLOCK]))
+        high = dot3((h[:, BLOCK:], l[:, BLOCK:]), (ph[BLOCK:, BLOCK:], plo[BLOCK:, BLOCK:]))
+        for g in range(4):
+            store(g, low[:, g * 128 : (g + 1) * 128])
+            store(g + 4, high[:, g * 128 : (g + 1) * 128])
+
+    def direct(i):
+        @pl.when(chip_lower)
+        def _():
+            here = slice(i * 128, (i + 1) * 128)
+
+            def store(g, value):
+                yp[g % 2, g // 2, here, :] = value
+
+            mapped(mf[here, :], store)
+
+    swap = push(yp.at[1 - k], q0, a0, b0, sibling)
+
+    def spread(d):
+        return push(yp.at[k, py[d]], q1.at[d], a1.at[d], b1s.at[d], (z, x, py[d], k))
+
+    def swap_start():
+        @pl.when(chip_lower)
+        def _():
+            swap.start()
+
+    def swap_end():
+        @pl.when(chip_lower)
+        def _():
+            swap.wait()
+            yp[pl.ds(k, 1)] += q0[...][None]
+            for d in range(3):
+                spread(d).start()
+
+    def scatter(d, i):
+        here = pl.ds(pl.multiple_of(i * 128, 128), 128)
+        to = pc[d]
+        return push(tq.at[to, here, :], rt.at[here, :], es.at[d, i], er.at[i], (z, x, to >> 1, to & 1))
+
+    def last_part(i):
+        here = pl.ds(pl.multiple_of(i * 128, 128), 128)
+
+        def store(g, value):
+            tq[g, here, :] = value
+
+        mapped(t[here, :], store)
+        for d in range(7):
+            scatter(d, i).start()
+
+    def chain(s):
+        i = s - 2 * position
+
+        @pl.when(taking & (i >= 0) & (i < CHUNKS))
+        def _():
+            here = pl.ds(pl.multiple_of(i * LINES, LINES), LINES)
+
             @pl.when(position > 0)
             def _():
                 chunk(i).wait_recv()
@@ -405,59 +479,15 @@
 
             @pl.when(jnp.logical_not(last))
             def _():
+                @pl.when(i >= 2)
+                def _():
+                    chunk(i - 2).wait_send()
+
                 chunk(i).start()
 
-    def mapped(part_rows, store):
-        h, l = split(part_rows)
-        for g in range(8):
-            cols = slice(g * 128, (g + 1) * 128)
-            at = 0 if g < 4 else BLOCK
-            store(g, dot3((h[:, at:], l[:, at:]), (ph[at:, cols], plo[at:, cols])))
-
-    def direct(i):
-        @pl.when(chip_lower)
-        def _():
-            here = slice(i * 128, (i + 1) * 128)
-
-            def store(g, value):
-                yp[g % 2, g // 2, here, :] = value
-
-            mapped(mf[here, :], store)
-
-    swap = push(yp.at[1 - k], q0, a0, b0, sibling)
-
-    def spread(d):
-        return push(yp.at[k, py[d]], q1.at[d], a1.at[d], b1s.at[d], (z, x, py[d], k))
-
-    def swap_start():
-        @pl.when(chip_lower)
-        def _():
-            swap.start()
-
-    def swap_end():
-        @pl.when(chip_lower)
-        def _():
-            swap.wait()
-            yp[pl.ds(k, 1)] += q0[...][None]
-            for d in range(3):
-                spread(d).start()
-
-    def scatter(d, i):
-        here = pl.ds(i * 128, 128)
-        to = pc[d]
-        return push(tq.at[to, here, :], rt.at[here, :], es.at[d, i], er.at[i], (z, x, to >> 1, to & 1))
-
-    def last_part(i):
-        @pl.when(last)
-        def _():
-            here = slice(i * 128, (i + 1) * 128)
-
-            def store(g, value):
-                tq[g, here, :] = value
-
-            mapped(t[here, :], store)
-            for d in range(7):
-                scatter(d, i).start()
+            @pl.when(last & (lax.rem(i, 4) == 3))
+            def _():
+                last_part(i >> 2)
 
     def sum_one():
         finish(c1)
@@ -483,27 +513,40 @@
 
         return run
 
+    def gather_one():
+        finish(c5)
+        start(c6)
+        c7[0].start()
+
+    def gather_two():
+        for d in range(3):
+            c6[d].wait_recv()
+            c7[d + 1].start()
+
     beside = {
-        0: [sum_one],
-        1: [lambda: direct(0)],
-        2: [sum_two],
-        3: [lambda: direct(1)],
-        4: [sum_three],
-        5: [lambda: direct(2)],
-        6: [then(c4, c5)],
-        7: [lambda: direct(3), swap_start],
-        8: [then(c5, c6)],
-        9: [swap_end],
-        10: [pre_three],
-        11: [then(c6, c7)],
+        1: lambda: direct(0),
+        3: sum_one,
+        4: lambda: direct(1),
+        6: sum_two,
+        7: lambda: direct(2),
+        9: sum_three,
+        10: lambda: direct(3),
+        11: swap_start,
+        12: then(c4, c5),
+        13: pre_three,
+        15: gather_one,
+        17: swap_end,
+        21: gather_two,
     }
-    for i in range(CHUNKS):
-        chain(i)
-        if i % 4 == 3:
-            last_part(i // 4)
-        for step in beside.get(i, []):
-            step()
-
+
+    @pl.loop(0, CHUNKS + 14)
+    def _(s):
+        chain(s)
+        for at, step in beside.items():
+            pl.when(s == at)(step)
+
+    for copy in c0 + c6:
+        copy.wait_send()
     finish(c7)
 
     def load(block):
@@ -563,10 +606,12 @@
     def _():
         @pl.loop(0, HOPS)
         def _(i):
+            beside_own(i).wait_send()
+            beside_other(i).wait_send()
+
+        for i in (HOPS - 2, HOPS - 1):
             first_hop(0, i).wait_send()
             first_hop(1, i).wait_send()
-            beside_own(i).wait_send()
-            beside_other(i).wait_send()
 
         for i in range(4):
             for d in range(7):
@@ -589,7 +634,7 @@
 
     @pl.when(taking & jnp.logical_not(last))
     def _():
-        for i in range(CHUNKS):
+        for i in (CHUNKS - 2, CHUNKS - 1):
             chunk(i).wait_send()
 
     @pl.when(chip_lower)
@@ -642,8 +687,8 @@
             pltpu.VMEM((8, BLOCK, 128), F32),
             pltpu.VMEM((BLOCK, 128), F32),
             dma((10,)), dma((2, HOPS)), dma((HOPS,)), dma((2, HOPS)), dma((HOPS,)), dma((3,)), dma((3,)),
-            dma, dma, dma((3,)), dma((3,)), dma((3,)), dma((3,)), dma((7,)), dma((7,)),
-            dma((7,)), dma((7,)), dma((3,)), dma((3,)), dma((3,)), dma((3,)), dma, dma,
+            dma((4,)), dma((4,)), dma((3,)), dma((3,)), dma((3,)), dma((3,)), dma((7,)), dma((7,)),
+            dma((7,)), dma((7,)), dma((3,)), dma((3,)), dma((3,)), dma((3,)), dma((4,)), dma((4,)),
             dma((CHUNKS,)), dma((CHUNKS,)), dma, dma, dma((3,)), dma((3,)), dma((7, 4)), dma((4,)),
         ],
         compiler_params=pltpu.CompilerParams(

time: 204 us -> 151 us (0.74)
  Pallas kernels: 196 us -> 144 us
    pallas_call x1, Pallas kernels: 196 us -> 144 us  [shards(): pl.pallas_call(kernel, name='adjoint', out_shape=(shape((BLOCK, 128), F32...]
where the time goes in v3:
time: 151 us; the launch traced here: 149 us
  Pallas kernels  144 us (95%)
  local copies, waits for them, and re-layouts  4.91 us (3%)
    pallas_call x1, Pallas kernels, shards(): pl.pallas_call(kernel, name='adjoint', out_shape=(shape((BLOCK, 128), F32...  144 us
    unnamed x3, local copies, waits for them, and re-layouts  4.91 us

profile of v3, /device:TPU:2, one launch (start us, length us, event | category | flops | bytes accessed | tf_op | source)
XLA Modules:
  0.0 149.2 jit_solution(6062768085217983496)
XLA Ops:
  0.6 143.7 %adjoint.1 = (f32[512,128]{1,0:T(8,128)}, f32[64,512]{1,0:T(8,128)}, f32[2,64,512]{2,1,0:T(8,128)}) custom-call(bf16[512,2048]{1,0:T(8,128)(2,1)} %trail.1, bf16[2048,1024]{1,0:T(8,128)(2,1)} %fac.1, bf16[512,512]{1,0:T(8,128)(2,1)} %xf.1, bf16[2,512,512]{2,1,0:T(8,128)(2,1)} %lf.1, f32[2,512,512]{2,1,0:T(8,128)} %li.1, bf16[512,1024]{1,0:T(8,128)(2,1)} %grad.1, ...), custom_call_target="tpu_custom_call" | custom-call | tf_op jit(solution)/shard_map/adjoint/pallas_call | solution.py:652
  144.3 1.7 %copy.14 = f32[512,128]{1,0:T(8,128)} copy(f32[512,128]{1,0:T(8,128)} %get-tuple-element.6) | data formatting | bytes 524288
  146.0 1.6 %copy.15 = f32[64,512]{1,0:T(8,128)} copy(f32[64,512]{1,0:T(8,128)} %get-tuple-element.7) | data formatting | bytes 262144
  147.6 1.7 %copy.16 = f32[2,64,512]{2,1,0:T(8,128)} copy(f32[2,64,512]{2,1,0:T(8,128)} %get-tuple-element.8) | data formatting | bytes 524288

commit v4 on v3

--- a/solution.py
+++ b/solution.py
@@ -64,7 +64,8 @@
     scale = jnp.where(cols < rows, 1.0, jnp.where(cols == rows, 0.5, 0.0))
     return (m.astype(F32) * scale).astype(BF16)
 
-CHUNKS = 16
+CHUNKS = 32
+SKEW = 4
 LINES = BLOCK // CHUNKS
 HOPS = 16
 
@@ -165,6 +166,9 @@
         )
 
     def feed(lo, hi):
+        if lo >= HOPS:
+            return
+
         @pl.when(last)
         def _():
             @pl.loop(lo, min(hi, HOPS))
@@ -219,9 +223,10 @@
         get_trail.wait()
         get_factor.wait()
 
-        @pl.loop(0, 4)
-        def _(i):
-            here = pl.ds(pl.multiple_of(i * 128, 128), 128)
+    def product(i):
+        @pl.when(lower)
+        def _():
+            here = slice(i * 128, (i + 1) * 128)
 
             @pl.when(last)
             def _():
@@ -235,18 +240,15 @@
         w[...] = jnp.zeros_like(w)
         t[...] = jnp.zeros_like(t)
 
+    for i in range(4):
+        relays(i, i + 1)
+        product(i)
+
     get_grad.wait()
 
     @pl.when(last)
     def _():
         get_source.wait()
-
-    relays(0, 4)
-    others(0, 4)
-
-    @pl.when(lower)
-    def _():
-        f[...] = fz[mine, :]
 
     own = jnp.where(last, 1.0, 0.0)
 
@@ -261,12 +263,6 @@
             value = dot2(split(ga - mfa), fb, 0, 0) - dot2(fa, split(mfb), 0, 0)
             for j in range(4):
                 w[pl.ds(j * 1536 + block * BLOCK, BLOCK), :] = value[:, j * 128 : (j + 1) * 128]
-
-    add_block(0, 1, 1)
-    relays(4, 6)
-    add_block(1, 1, 0)
-    relays(6, 8)
-    add_block(2, 0, 0)
 
     half = k * 3072
     first = jnp.where(k == 0, y, x)
@@ -323,17 +319,12 @@
     c7 = [
         whole(half + lax.rem(first + 4 - j, 4) * 768, 768, g0.at[j], u0.at[j], sibling) for j in range(4)
     ]
-    start(c0)
-
     def pre_one():
         finish(get_small)
-        li0, li1 = split(liv[0]), split(liv[1])
-        ph[0:BLOCK, 0:BLOCK], plo[0:BLOCK, 0:BLOCK] = li0
-        ph[BLOCK:, BLOCK:], plo[BLOCK:, BLOCK:] = li1
+        ph[0:BLOCK, 0:BLOCK], plo[0:BLOCK, 0:BLOCK] = split(liv[0])
+        ph[BLOCK:, BLOCK:], plo[BLOCK:, BLOCK:] = split(liv[1])
         ph[0:BLOCK, BLOCK:] = jnp.zeros((BLOCK, BLOCK), BF16)
         plo[0:BLOCK, BLOCK:] = jnp.zeros((BLOCK, BLOCK), BF16)
-        high, low = split(dot3(split(dot2(li1, xv[...])), li0))
-        ph[BLOCK:, 0:BLOCK], plo[BLOCK:, 0:BLOCK] = -high, -low
 
     def li0():
         return ph[0:BLOCK, 0:BLOCK], plo[0:BLOCK, 0:BLOCK]
@@ -350,9 +341,20 @@
     def keep(n, value):
         pairs[2 * n], pairs[2 * n + 1] = split(value)
 
-    def pre_two():
+    def pre_cross():
+        keep(0, dot2(li1(), xv[...]))
+
+    def pre_b1():
+        high, low = split(dot3(pair(0), li0()))
+        ph[BLOCK:, 0:BLOCK], plo[BLOCK:, 0:BLOCK] = -high, -low
+
+    def pre_j0():
         keep(0, dot2(li0(), lfv[0]))
+
+    def pre_j1():
         keep(1, dot2(li1(), lfv[1]))
+
+    def pre_b2():
         keep(2, -dot2(minus_b1(), lfv[0]))
 
     def pre_three():
@@ -383,25 +385,39 @@
                 else:
                     t[lines, :] += value
 
-    pre_one()
-    relays(8, 9)
-    transposed(0)
-    relays(9, 10)
-    pre_two()
-    relays(10, 11)
+    def ready():
+        others(0, 4)
+
+        @pl.when(lower)
+        def _():
+            f[...] = fz[mine, :]
+
+    between = {
+        4: [pre_one],
+        5: [pre_cross],
+        6: [pre_b1],
+        7: [ready, lambda: add_block(0, 1, 1)],
+        8: [lambda: add_block(1, 1, 0)],
+        9: [lambda: add_block(2, 0, 0), lambda: start(c0)],
+        10: [pre_j0],
+        11: [pre_j1],
+        12: [pre_b2],
+        13: [lambda: others(4, 8)],
+        14: [lambda: transposed(0)],
+    }
+    for i in range(4, HOPS):
+        relays(i, i + 1)
+        for piece in between.get(i, []):
+            piece()
     for j in range(4):
         c0[j].wait_recv()
         here = quarter(half, first + 1 + j)
         w[here, :] += full[here, :]
         if j < 3:
             c1[j].start()
-    relays(11, 12)
-    others(4, 8)
     transposed(1)
-    relays(12, 14)
     others(8, 12)
     transposed(2)
-    relays(14, 16)
     others(12, 16)
     transposed(3)
 
@@ -466,7 +482,7 @@
             scatter(d, i).start()
 
     def chain(s):
-        i = s - 2 * position
+        i = s - SKEW * position
 
         @pl.when(taking & (i >= 0) & (i < CHUNKS))
         def _():
@@ -479,15 +495,15 @@
 
             @pl.when(jnp.logical_not(last))
             def _():
-                @pl.when(i >= 2)
+                @pl.when(i >= 4)
                 def _():
-                    chunk(i - 2).wait_send()
+                    chunk(i - 4).wait_send()
 
                 chunk(i).start()
 
-            @pl.when(last & (lax.rem(i, 4) == 3))
+            @pl.when(last & (lax.rem(i, 8) == 7))
             def _():
-                last_part(i >> 2)
+                last_part(i >> 3)
 
     def sum_one():
         finish(c1)
@@ -525,21 +541,21 @@
 
     beside = {
         1: lambda: direct(0),
-        3: sum_one,
         4: lambda: direct(1),
-        6: sum_two,
         7: lambda: direct(2),
-        9: sum_three,
         10: lambda: direct(3),
         11: swap_start,
-        12: then(c4, c5),
-        13: pre_three,
-        15: gather_one,
-        17: swap_end,
-        21: gather_two,
+        13: sum_one,
+        19: sum_two,
+        22: swap_end,
+        25: sum_three,
+        28: pre_three,
+        31: then(c4, c5),
+        37: gather_one,
+        51: gather_two,
     }
 
-    @pl.loop(0, CHUNKS + 14)
+    @pl.loop(0, CHUNKS + 7 * SKEW)
     def _(s):
         chain(s)
         for at, step in beside.items():
@@ -634,13 +650,17 @@
 
     @pl.when(taking & jnp.logical_not(last))
     def _():
-        for i in (CHUNKS - 2, CHUNKS - 1):
+        for i in range(CHUNKS - 4, CHUNKS):
             chunk(i).wait_send()
 
     @pl.when(chip_lower)
     def _():
         for d in range(3):
             spread(d).wait_send()
+
+
+def copy_kernel(a, b, c, out_a, out_b, out_c):
+    out_a[...], out_b[...], out_c[...] = a[...], b[...], c[...]
 
 
 def shards(trail, fac, xf, lf, li, grad, cg, dg):
@@ -649,12 +669,13 @@
     vmem = pl.BlockSpec(memory_space=pltpu.VMEM)
     shape = jax.ShapeDtypeStruct
     square = (BLOCK, BLOCK)
-    return pl.pallas_call(
+    results = (
+        shape((BLOCK, 128), F32), shape((64, BLOCK), F32), shape((2, 64, BLOCK), F32),
+    )
+    made = pl.pallas_call(
         kernel,
         name="adjoint",
-        out_shape=(
-            shape((BLOCK, 128), F32), shape((64, BLOCK), F32), shape((2, 64, BLOCK), F32),
-        ),
+        out_shape=results,
         in_specs=[anywhere] * 8,
         out_specs=[vmem] * 3,
         scratch_shapes=[
@@ -695,6 +716,9 @@
             collective_id=0, has_side_effects=True, vmem_limit_bytes=VMEM_BYTES
         ),
     )(trail, fac, xf, lf, li, grad, cg, dg)
+    return pl.pallas_call(
+        copy_kernel, name="results", out_shape=results, in_specs=[vmem] * 3, out_specs=[vmem] * 3
+    )(*made)
 
 
 def solution(mesh):

time: 151 us -> 126 us (0.83)
  Pallas kernels: 144 us -> 125 us
  local copies, waits for them, and re-layouts: 4.91 us -> 0 us
    pallas_call x1 -> x2, Pallas kernels: 144 us -> 125 us  [the longest x1 123 us: shards(): pl.pallas_call(kernel, name='adjoint', out_shape=results, in_specs=[anywh...]
    unnamed x3 -> x0, local copies, waits for them, and re-layouts: 4.91 us -> none
where the time goes in v4:
time: 126 us; the launch traced here: 125 us
  Pallas kernels  125 us (99%)
    pallas_call x1, Pallas kernels, shards(): pl.pallas_call(kernel, name='adjoint', out_shape=results, in_specs=[anywh...  123 us

profile of v4, /device:TPU:2, one launch (start us, length us, event | category | flops | bytes accessed | tf_op | source)
XLA Modules:
  0.0 125.2 jit_solution(17100455792914636903)
XLA Ops:
  0.6 122.6 %adjoint.1 = (f32[512,128]{1,0:T(8,128)}, f32[64,512]{1,0:T(8,128)}, f32[2,64,512]{2,1,0:T(8,128)}) custom-call(bf16[512,2048]{1,0:T(8,128)(2,1)} %trail.1, bf16[2048,1024]{1,0:T(8,128)(2,1)} %fac.1, bf16[512,512]{1,0:T(8,128)(2,1)} %xf.1, bf16[2,512,512]{2,1,0:T(8,128)(2,1)} %lf.1, f32[2,512,512]{2,1,0:T(8,128)} %li.1, bf16[512,1024]{1,0:T(8,128)(2,1)} %grad.1, ...), custom_call_target="tpu_custom_call" | custom-call | tf_op jit(solution)/shard_map/adjoint/pallas_call | solution.py:675
  123.3 1.9 %results.1 = (f32[512,128]{1,0:T(8,128)}, f32[64,512]{1,0:T(8,128)}, f32[2,64,512]{2,1,0:T(8,128)}) custom-call(f32[512,128]{1,0:T(8,128)} %get-tuple-element.6.a, f32[64,512]{1,0:T(8,128)} %get-tuple-element.7.b, f32[2,64,512]{2,1,0:T(8,128)} %get-tuple-element.8.c), custom_call_target="tpu_custom_call" | custom-call | tf_op jit(solution)/shard_map/results/pallas_call | solution.py:719

commit v5 on v4

--- a/solution.py
+++ b/solution.py
@@ -319,6 +319,11 @@
     c7 = [
         whole(half + lax.rem(first + 4 - j, 4) * 768, 768, g0.at[j], u0.at[j], sibling) for j in range(4)
     ]
+    def sum_one():
+        finish(c1)
+        w[part(at1, 768), :] += r1[0] + r1[1] + r1[2]
+        start(c2)
+
     def pre_one():
         finish(get_small)
         ph[0:BLOCK, 0:BLOCK], plo[0:BLOCK, 0:BLOCK] = split(liv[0])
@@ -392,31 +397,30 @@
         def _():
             f[...] = fz[mine, :]
 
+    def pass_on(j):
+        c0[j].wait_recv()
+        here = quarter(half, first + 1 + j)
+        w[here, :] += full[here, :]
+        if j < 3:
+            c1[j].start()
+
     between = {
-        4: [pre_one],
-        5: [pre_cross],
-        6: [pre_b1],
         7: [ready, lambda: add_block(0, 1, 1)],
         8: [lambda: add_block(1, 1, 0)],
         9: [lambda: add_block(2, 0, 0), lambda: start(c0)],
-        10: [pre_j0],
-        11: [pre_j1],
-        12: [pre_b2],
-        13: [lambda: others(4, 8)],
+        10: [pre_one],
+        11: [lambda: pass_on(0), lambda: pass_on(1)],
+        12: [lambda: pass_on(2), lambda: pass_on(3), pre_cross],
+        13: [lambda: others(4, 8), pre_b1],
         14: [lambda: transposed(0)],
     }
     for i in range(4, HOPS):
         relays(i, i + 1)
         for piece in between.get(i, []):
             piece()
-    for j in range(4):
-        c0[j].wait_recv()
-        here = quarter(half, first + 1 + j)
-        w[here, :] += full[here, :]
-        if j < 3:
-            c1[j].start()
     transposed(1)
     others(8, 12)
+    sum_one()
     transposed(2)
     others(12, 16)
     transposed(3)
@@ -505,11 +509,6 @@
             def _():
                 last_part(i >> 3)
 
-    def sum_one():
-        finish(c1)
-        w[part(at1, 768), :] += r1[0] + r1[1] + r1[2]
-        start(c2)
-
     def sum_two():
         finish(c2)
         w[part(at2, 192), :] += r2[0] + r2[1] + r2[2]
@@ -539,20 +538,96 @@
             c6[d].wait_recv()
             c7[d + 1].start()
 
+    def square(n):
+        return pl.ds(n // 2 * BLOCK, BLOCK), pl.ds(n % 2 * BLOCK, BLOCK)
+
+    def hold(n, value):
+        fv[square(2 * n)], fv[square(2 * n + 1)] = split(value)
+
+    def held(n):
+        return fv[square(2 * n)], fv[square(2 * n + 1)]
+
+    def total(block):
+        return jnp.concatenate(
+            [full[pl.ds(j * 1536 + block * BLOCK, BLOCK), :] for j in range(4)], axis=1
+        )
+
+    slab = pl.ds(pl.multiple_of(c * 64, 64), 64)
+
+    def turned(parts):
+        pick = jnp.where(
+            lax.broadcasted_iota(jnp.int32, (BLOCK, 64), 0)
+            == c * 64 + lax.broadcasted_iota(jnp.int32, (BLOCK, 64), 1),
+            1.0,
+            0.0,
+        ).astype(BF16)
+        return tuple(dot(pick, part_of, 0, 1).astype(BF16) for part_of in parts)
+
+    def dense_one():
+        hold(0, symmetric(consts[1] - dot3(pair(1), split(total(0)), 0, 0)))
+
+    def dense_two():
+        hold(1, total(1))
+        mf[:, 0:BLOCK] = dot3(held(1), pair(0))
+
+    def dense_three():
+        hold(2, mf[:, 0:BLOCK] + dot3(held(0), pair(2)))
+
+    def dense_four():
+        hold(3, consts[2] - dot3(li1(), held(2), 0, 0))
+
+    def dense_five():
+        mf[:, BLOCK:] = consts[0] - dot3(pair(0), split(total(2)), 0, 0)
+
+    def dense_six():
+        mf[:, BLOCK:] += dot3(pair(2), held(1), 0, 0)
+
+    def dense_seven():
+        hold(2, symmetric(mf[:, BLOCK:] - dot2(held(3), xv[...], 0, 0)))
+
+    def dense_eight():
+        lit1 = turned(li1())
+        ls1 = split(dot3(lit1, held(0)))
+        diag_out[1] = dot3(ls1, li1())
+        cross_out[...] = dot2(cgv[slab, :], li0()) - (
+            dot3(split(dot3(lit1, held(1))), li0()) - dot3(ls1, minus_b1())
+        )
+
+    def dense_nine():
+        diag_out[0] = dot3(split(dot3(turned(li0()), held(2))), li0())
+
+    cols = pl.ds(pl.multiple_of(c * 128, 128), 128)
+
+    def own_gradient():
+        panel_out[...] = dot2(gv[...], (ph[:, cols], plo[:, cols]))
+
     beside = {
+        0: sum_two,
         1: lambda: direct(0),
-        4: lambda: direct(1),
+        3: lambda: direct(1),
+        6: sum_three,
         7: lambda: direct(2),
-        10: lambda: direct(3),
-        11: swap_start,
-        13: sum_one,
-        19: sum_two,
+        9: lambda: direct(3),
+        10: swap_start,
+        12: then(c4, c5),
+        14: pre_j0,
+        16: pre_j1,
+        18: gather_one,
+        20: pre_b2,
         22: swap_end,
-        25: sum_three,
-        28: pre_three,
-        31: then(c4, c5),
-        37: gather_one,
-        51: gather_two,
+        25: pre_three,
+        28: own_gradient,
+        33: gather_two,
+        37: then(c7, []),
+        38: dense_one,
+        40: dense_two,
+        42: dense_three,
+        44: dense_four,
+        46: dense_five,
+        48: dense_six,
+        50: dense_seven,
+        52: dense_eight,
+        54: dense_nine,
     }
 
     @pl.loop(0, CHUNKS + 7 * SKEW)
@@ -563,41 +638,6 @@
 
     for copy in c0 + c6:
         copy.wait_send()
-    finish(c7)
-
-    def load(block):
-        return split(
-            jnp.concatenate([full[pl.ds(j * 1536 + block * BLOCK, BLOCK), :] for j in range(4)], axis=1)
-        )
-
-    w11, w10, w00 = load(0), load(1), load(2)
-    slab = pl.ds(pl.multiple_of(c * 64, 64), 64)
-    pick = jnp.where(
-        lax.broadcasted_iota(jnp.int32, (BLOCK, 64), 0)
-        == c * 64 + lax.broadcasted_iota(jnp.int32, (BLOCK, 64), 1),
-        1.0,
-        0.0,
-    ).astype(BF16)
-
-    def turned(parts):
-        return tuple(dot(pick, part_of, 0, 1).astype(BF16) for part_of in parts)
-
-    lit1, lit0 = turned(li1()), turned(li0())
-    sym1 = split(symmetric(consts[1] - dot3(pair(1), w11, 0, 0)))
-    inner = split(dot3(w10, pair(0)) + dot3(sym1, pair(2)))
-    cl = split(consts[2] - dot3(li1(), inner, 0, 0))
-    g_zero = consts[0] - dot3(pair(0), w00, 0, 0) + dot3(pair(2), w10, 0, 0) - dot2(cl, xv[...], 0, 0)
-    sym0 = split(symmetric(g_zero))
-    ls1 = split(dot3(lit1, sym1))
-    diag_out[1] = dot3(ls1, li1())
-    cross_out[...] = dot2(cgv[slab, :], li0()) - (
-        dot3(split(dot3(lit1, w10)), li0()) - dot3(ls1, minus_b1())
-    )
-    diag_out[0] = dot3(split(dot3(lit0, sym0)), li0())
-
-    cols = pl.ds(pl.multiple_of(c * 128, 128), 128)
-    panel_out[...] = dot2(gv[...], (ph[:, cols], plo[:, cols]))
-
     @pl.when(chip_lower)
     def _():
         panel_out[...] -= yp[k, y]

time: 126 us -> 137 us (1.087)
  Pallas kernels: 125 us -> 134 us
    pallas_call x1, Pallas kernels: 123 us -> 132 us  [shards(): pl.pallas_call(kernel, name='adjoint', out_shape=results, in_specs=[anywh...]
where the time goes in v5:
time: 137 us; the launch traced here: 135 us
  Pallas kernels  134 us (98%)
    pallas_call x1, Pallas kernels, shards(): pl.pallas_call(kernel, name='adjoint', out_shape=results, in_specs=[anywh...  132 us

profile of v5, /device:TPU:2, one launch (start us, length us, event | category | flops | bytes accessed | tf_op | source)
XLA Modules:
  0.0 135.0 jit_solution(5434508902860449809)
XLA Ops:
  0.6 132.4 %adjoint.1 = (f32[512,128]{1,0:T(8,128)}, f32[64,512]{1,0:T(8,128)}, f32[2,64,512]{2,1,0:T(8,128)}) custom-call(bf16[512,2048]{1,0:T(8,128)(2,1)} %trail.1, bf16[2048,1024]{1,0:T(8,128)(2,1)} %fac.1, bf16[512,512]{1,0:T(8,128)(2,1)} %xf.1, bf16[2,512,512]{2,1,0:T(8,128)(2,1)} %lf.1, f32[2,512,512]{2,1,0:T(8,128)} %li.1, bf16[512,1024]{1,0:T(8,128)(2,1)} %grad.1, ...), custom_call_target="tpu_custom_call" | custom-call | tf_op jit(solution)/shard_map/adjoint/pallas_call | solution.py:715
  133.1 1.9 %results.1 = (f32[512,128]{1,0:T(8,128)}, f32[64,512]{1,0:T(8,128)}, f32[2,64,512]{2,1,0:T(8,128)}) custom-call(f32[512,128]{1,0:T(8,128)} %get-tuple-element.6.a, f32[64,512]{1,0:T(8,128)} %get-tuple-element.7.b, f32[2,64,512]{2,1,0:T(8,128)} %get-tuple-element.8.c), custom_call_target="tpu_custom_call" | custom-call | tf_op jit(solution)/shard_map/results/pallas_call | solution.py:759

commit v6 on v5

--- a/solution.py
+++ b/solution.py
@@ -420,7 +420,6 @@
             piece()
     transposed(1)
     others(8, 12)
-    sum_one()
     transposed(2)
     others(12, 16)
     transposed(3)
@@ -602,32 +601,23 @@
         panel_out[...] = dot2(gv[...], (ph[:, cols], plo[:, cols]))
 
     beside = {
-        0: sum_two,
-        1: lambda: direct(0),
-        3: lambda: direct(1),
-        6: sum_three,
-        7: lambda: direct(2),
-        9: lambda: direct(3),
-        10: swap_start,
-        12: then(c4, c5),
-        14: pre_j0,
-        16: pre_j1,
-        18: gather_one,
-        20: pre_b2,
-        22: swap_end,
-        25: pre_three,
-        28: own_gradient,
-        33: gather_two,
-        37: then(c7, []),
-        38: dense_one,
-        40: dense_two,
-        42: dense_three,
-        44: dense_four,
-        46: dense_five,
-        48: dense_six,
-        50: dense_seven,
-        52: dense_eight,
-        54: dense_nine,
+        1: sum_one,
+        2: lambda: direct(0),
+        4: lambda: direct(1),
+        7: sum_two,
+        8: lambda: direct(2),
+        10: lambda: direct(3),
+        11: swap_start,
+        13: sum_three,
+        15: pre_j0,
+        17: pre_j1,
+        19: then(c4, c5),
+        21: pre_b2,
+        23: swap_end,
+        25: gather_one,
+        29: pre_three,
+        33: own_gradient,
+        41: gather_two,
     }
 
     @pl.loop(0, CHUNKS + 7 * SKEW)
@@ -638,6 +628,12 @@
 
     for copy in c0 + c6:
         copy.wait_send()
+    finish(c7)
+    for step in (
+        dense_one, dense_two, dense_three, dense_four, dense_five, dense_six, dense_seven,
+        dense_eight, dense_nine,
+    ):
+        step()
     @pl.when(chip_lower)
     def _():
         panel_out[...] -= yp[k, y]

time: 137 us -> 139 us (1.015); the launches traced: 135 us -> 139 us
  Pallas kernels: 134 us -> 138 us
    pallas_call x1, Pallas kernels: 132 us -> 137 us  [shards(): pl.pallas_call(kernel, name='adjoint', out_shape=results, in_specs=[anywh...]
where the time goes in v6:
time: 139 us
  Pallas kernels  138 us (99%)
    pallas_call x1, Pallas kernels, shards(): pl.pallas_call(kernel, name='adjoint', out_shape=results, in_specs=[anywh...  137 us

profile of v6, /device:TPU:2, one launch (start us, length us, event | category | flops | bytes accessed | tf_op | source)
XLA Modules:
  0.0 139.1 jit_solution(9316492135736551858)
XLA Ops:
  0.6 136.5 %adjoint.1 = (f32[512,128]{1,0:T(8,128)}, f32[64,512]{1,0:T(8,128)}, f32[2,64,512]{2,1,0:T(8,128)}) custom-call(bf16[512,2048]{1,0:T(8,128)(2,1)} %trail.1, bf16[2048,1024]{1,0:T(8,128)(2,1)} %fac.1, bf16[512,512]{1,0:T(8,128)(2,1)} %xf.1, bf16[2,512,512]{2,1,0:T(8,128)(2,1)} %lf.1, f32[2,512,512]{2,1,0:T(8,128)} %li.1, bf16[512,1024]{1,0:T(8,128)(2,1)} %grad.1, ...), custom_call_target="tpu_custom_call" | custom-call | tf_op jit(solution)/shard_map/adjoint/pallas_call | solution.py:711
  137.2 1.9 %results.1 = (f32[512,128]{1,0:T(8,128)}, f32[64,512]{1,0:T(8,128)}, f32[2,64,512]{2,1,0:T(8,128)}) custom-call(f32[512,128]{1,0:T(8,128)} %get-tuple-element.6.a, f32[64,512]{1,0:T(8,128)} %get-tuple-element.7.b, f32[2,64,512]{2,1,0:T(8,128)} %get-tuple-element.8.c), custom_call_target="tpu_custom_call" | custom-call | tf_op jit(solution)/shard_map/results/pallas_call | solution.py:755

commit v7 on v4

--- a/solution.py
+++ b/solution.py
@@ -545,14 +545,14 @@
         7: lambda: direct(2),
         10: lambda: direct(3),
         11: swap_start,
-        13: sum_one,
-        19: sum_two,
+        9: sum_one,
+        14: sum_two,
         22: swap_end,
-        25: sum_three,
+        19: sum_three,
         28: pre_three,
-        31: then(c4, c5),
-        37: gather_one,
-        51: gather_two,
+        24: then(c4, c5),
+        30: gather_one,
+        46: gather_two,
     }
 
     @pl.loop(0, CHUNKS + 7 * SKEW)

time: 126 us -> 129 us (1.024); the launches traced: 125 us -> 127 us
    pallas_call x1, Pallas kernels: 123 us -> 124 us  [shards(): pl.pallas_call(kernel, name='adjoint', out_shape=results, in_specs=[anywh...]
where the time goes in v7:
time: 129 us; the launch traced here: 127 us
  Pallas kernels  126 us (98%)
    pallas_call x1, Pallas kernels, shards(): pl.pallas_call(kernel, name='adjoint', out_shape=results, in_specs=[anywh...  124 us

profile of v7, /device:TPU:2, one launch (start us, length us, event | category | flops | bytes accessed | tf_op | source)
XLA Modules:
  0.0 126.9 jit_solution(2922813763656940330)
XLA Ops:
  0.6 124.3 %adjoint.1 = (f32[512,128]{1,0:T(8,128)}, f32[64,512]{1,0:T(8,128)}, f32[2,64,512]{2,1,0:T(8,128)}) custom-call(bf16[512,2048]{1,0:T(8,128)(2,1)} %trail.1, bf16[2048,1024]{1,0:T(8,128)(2,1)} %fac.1, bf16[512,512]{1,0:T(8,128)(2,1)} %xf.1, bf16[2,512,512]{2,1,0:T(8,128)(2,1)} %lf.1, f32[2,512,512]{2,1,0:T(8,128)} %li.1, bf16[512,1024]{1,0:T(8,128)(2,1)} %grad.1, ...), custom_call_target="tpu_custom_call" | custom-call | tf_op jit(solution)/shard_map/adjoint/pallas_call | solution.py:675
  125.0 1.9 %results.1 = (f32[512,128]{1,0:T(8,128)}, f32[64,512]{1,0:T(8,128)}, f32[2,64,512]{2,1,0:T(8,128)}) custom-call(f32[512,128]{1,0:T(8,128)} %get-tuple-element.6.a, f32[64,512]{1,0:T(8,128)} %get-tuple-element.7.b, f32[2,64,512]{2,1,0:T(8,128)} %get-tuple-element.8.c), custom_call_target="tpu_custom_call" | custom-call | tf_op jit(solution)/shard_map/results/pallas_call | solution.py:719
